TPU v7x, 128 devices: a whole 4x4x4 slice. The times are simulated.
128 devices in a mesh: tile: 16 (over z_lo, x, core), mode: 8 (over y, z_hi).
Axes of the slice: x: 4, y: 4, z: 4 (z_hi: 2, z_lo: 2; z = z_hi * 2 + z_lo), core: 2. Of those that a mesh axis runs over, the one named last changes fastest.
Arguments:
- object_field: float32 [2, 2, 4096, 384], P(None, None, 'tile'), may hold values from -4 to 4
- probe: float32 [8, 2, 256, 256], P('mode'), may hold values from -4 to 4
- measured: float32 [64, 256, 256], P('tile'), may hold values from 0 to 16
- prop_phase: float32 [256, 256], replicated, may hold values from -3.140625 to 3.140625
- counts: int32 [16], P('tile'), may hold values from 1 to 4, 32 in all
- row_offset: int32 [64], P('tile'), may hold values from 0 to 255
- col_offset: int32 [64], P('tile'), may hold values from 0 to 128
Outputs:
- object_grad: float32 [2, 2, 4096, 384], P(None, None, 'tile')
- probe_grad: float32 [8, 2, 256, 256], P('mode')
Inputs may be any that keep to these rules, and one draw needn't show every extreme that they name: Slot i is live for i % 4 < counts[i // 4]; some tile has all 4 slots live.
All inputs are finite; a program needn't handle non-finite values. No bound on the sum of `counts` on one device may be relied on, other than what follows from the above.
Results may differ from a plain program's by a relative error of at most 0.0003.
Values sent between devices are 32-bit elements; how exact they have to be, the bound alone decides.
No kernel may reach another device: no remote copies, remote signals or barrier semaphores. Data moves between devices by JAX's collectives and lax.ppermute only.
A program may use at most 128 MiB of HBM per device.

v0:
```python
import functools
import math

import jax
import jax.numpy as jnp
import numpy as np
from jax import lax
from jax.experimental import pallas as pl
from jax.experimental.pallas import tpu as pltpu
from jax.sharding import Mesh, PartitionSpec as P


WIN = 256
HALF = 128
MODES = 8
COLS = 384
F32 = jnp.float32
BF16 = jnp.bfloat16
TILE = ("zl", "x", "core")
MODE = ("y", "zh")
SPREAD = ("zl", "x", "y")
VMEM = pl.BlockSpec(memory_space=pltpu.VMEM)
SMEM = pl.BlockSpec(memory_space=pltpu.SMEM)
PARAMS = pltpu.CompilerParams(vmem_limit_bytes=24 * 1024 * 1024)


def make_tables():
    index = np.arange(HALF)
    angle = (index[:, None] * index[None, :] % HALF) * (2.0 * math.pi / HALF)
    cosine, sine = np.cos(angle) / 16.0, np.sin(angle) / 16.0
    ahead = np.block([[cosine, -sine], [sine, cosine]])
    both = []
    for matrix in (ahead, ahead.T):
        high = matrix.astype(np.float32).astype(jnp.bfloat16)
        low = (matrix - high.astype(np.float64)).astype(np.float32).astype(jnp.bfloat16)
        both += [high, low]
    turn = index * (math.pi / HALF)
    lane = np.stack([np.cos(turn), np.sin(turn)])
    lane_table = np.broadcast_to(lane[:, None, :], (2, 8, HALF)).astype(np.float32)
    row_table = np.broadcast_to(lane[:, :, None], (2, HALF, HALF)).astype(np.float32)
    order = np.concatenate([np.arange(0, WIN, 2), np.arange(1, WIN, 2)])
    pick = np.zeros((WIN, WIN), np.float32)
    pick[np.arange(WIN), order] = 1.0
    picks = np.stack([pick, pick.T]).astype(jnp.bfloat16)
    return np.stack(both), lane_table, row_table, picks


def mm(left, right):
    return jnp.dot(left, right, preferred_element_type=F32)


def split(value):
    high = value.astype(BF16)
    return high, (value - high.astype(F32)).astype(BF16)


def dot_right(value, tables, which):
    high, low = split(value)
    return mm(high, tables[which]) + (mm(low, tables[which]) + mm(high, tables[which + 1]))


def dot_left(tables, which, value):
    high, low = split(value)
    return mm(tables[which], high) + (mm(tables[which], low) + mm(tables[which + 1], high))


def right_forward(real, imag, tables, lane):
    rows = real.shape[0]
    cosine, sine = lane[0, 0:1, :], lane[1, 0:1, :]
    ar, br, ai, bi = real[:, :HALF], real[:, HALF:], imag[:, :HALF], imag[:, HALF:]
    dr, di = ar - br, ai - bi
    top = jnp.concatenate([ar + br, ai + bi], axis=1)
    low = jnp.concatenate([dr * cosine + di * sine, di * cosine - dr * sine], axis=1)
    out = dot_right(jnp.concatenate([top, low], axis=0), tables, 0)
    even, odd = out[:rows], out[rows:]
    return (
        jnp.concatenate([even[:, :HALF], odd[:, :HALF]], axis=1),
        jnp.concatenate([even[:, HALF:], odd[:, HALF:]], axis=1),
    )


def right_inverse(real, imag, tables, lane):
    rows = real.shape[0]
    cosine, sine = lane[0, 0:1, :], lane[1, 0:1, :]
    even = jnp.concatenate([real[:, :HALF], imag[:, :HALF]], axis=1)
    odd = jnp.concatenate([real[:, HALF:], imag[:, HALF:]], axis=1)
    out = dot_right(jnp.concatenate([even, odd], axis=0), tables, 2)
    er, ei = out[:rows, :HALF], out[:rows, HALF:]
    pr, pi = out[rows:, :HALF], out[rows:, HALF:]
    tr, ti = pr * cosine - pi * sine, pi * cosine + pr * sine
    return (
        jnp.concatenate([er + tr, er - tr], axis=1),
        jnp.concatenate([ei + ti, ei - ti], axis=1),
    )


def left_forward(real, imag, tables, row):
    width = real.shape[1]
    cosine, sine = row[0], row[1]
    ar, br, ai, bi = real[:HALF], real[HALF:], imag[:HALF], imag[HALF:]
    dr, di = ar - br, ai - bi
    top = jnp.concatenate([ar + br, ai + bi], axis=0)
    low = jnp.concatenate([dr * cosine + di * sine, di * cosine - dr * sine], axis=0)
    out = dot_left(tables, 2, jnp.concatenate([top, low], axis=1))
    even, odd = out[:, :width], out[:, width:]
    return (
        jnp.concatenate([even[:HALF], odd[:HALF]], axis=0),
        jnp.concatenate([even[HALF:], odd[HALF:]], axis=0),
    )


def left_inverse(real, imag, tables, row):
    width = real.shape[1]
    cosine, sine = row[0], row[1]
    even = jnp.concatenate([real[:HALF], imag[:HALF]], axis=0)
    odd = jnp.concatenate([real[HALF:], imag[HALF:]], axis=0)
    out = dot_left(tables, 0, jnp.concatenate([even, odd], axis=1))
    er, ei = out[:HALF, :width], out[HALF:, :width]
    pr, pi = out[:HALF, width:], out[HALF:, width:]
    tr, ti = pr * cosine - pi * sine, pi * cosine + pr * sine
    return (
        jnp.concatenate([er + tr, er - tr], axis=0),
        jnp.concatenate([ei + ti, ei - ti], axis=0),
    )


def times(ar, ai, br, bi):
    return ar * br - ai * bi, ar * bi + ai * br


def times_conj(ar, ai, br, bi):
    return ar * br + ai * bi, ar * bi - ai * br


BLOCKS = (slice(0, HALF), slice(HALF, WIN))


def cut_window(own, halo, row, col, out):
    rows = lax.broadcasted_iota(jnp.int32, (WIN, COLS), 0)
    lanes = lax.broadcasted_iota(jnp.int32, (WIN, HALF), 1)
    for part in range(2):
        chosen = jnp.where(rows < row, halo[part], own[part])
        first = jnp.where(lanes < col, chosen[:, 2 * HALF :], chosen[:, :HALF])
        ring = jnp.concatenate([first, chosen[:, HALF : 2 * HALF]], axis=1)
        ring = pltpu.roll(ring, lax.rem(WIN - row, WIN), 0)
        out[part] = pltpu.roll(ring, lax.rem(WIN - col, WIN), 1)


def prepare_kernel(place, measured, wave, picks, kernel_out, measured_out):
    def reorder(value):
        for side in range(2):
            high, _ = split(value)
            middle, low = split(value - high.astype(F32))
            if side == 0:
                value = mm(picks[0], high) + mm(picks[0], middle) + mm(picks[0], low)
            else:
                value = mm(high, picks[1]) + mm(middle, picks[1]) + mm(low, picks[1])
        return value

    kernel_out[0] = reorder(wave[0])
    kernel_out[1] = reorder(wave[1])
    measured_out[...] = reorder(measured[0])


def spread_mode(pair, window, prop, tables, lane, row_table, mid, out):
    for rows in BLOCKS:
        real, imag = pair(rows)
        real, imag = times(real, imag, window[0, rows, :], window[1, rows, :])
        real, imag = right_forward(real, imag, tables, lane)
        mid[0, rows, :] = real
        mid[1, rows, :] = imag
    for cols in BLOCKS:
        real, imag = left_forward(mid[0, :, cols], mid[1, :, cols], tables, row_table)
        real, imag = times(prop[0, :, cols], prop[1, :, cols], real, imag)
        real, imag = left_inverse(real, imag, tables, row_table)
        out[0, :, cols] = real
        out[1, :, cols] = imag


def start_kernel(place, row_off, col_off, own, halo, probe, prop, tables, lane, row_table,
                 moved, probes, window, mid):
    slot = place[0]
    cut_window(own.at[0], halo, row_off[slot], col_off[slot], window)
    probes[0] = probe[0]
    spread_mode(lambda rows: (probe[0, 0, rows, :], probe[0, 1, rows, :]), window, prop, tables,
                lane, row_table, mid, moved.at[0])


def first_kernel(place, window, mine, other, prop, tables, lane, row_table, moved_in, probes_in,
                 moved, probes, mid):
    core = place[2]

    def pair(rows):
        index = BLOCKS.index(rows)
        values = []
        for part in range(2):
            value = jnp.where(core == index, mine[0, part], other[0, part])
            probes[0, part, rows, :] = value
            values.append(value)
        return values

    spread_mode(pair, window, prop, tables, lane, row_table, mid, moved.at[0])


def second_kernel(place, row_off, col_off, own, halo, moved, tables, lane, row_table,
                  before, far, power, window, mid):
    slot = place[0]

    @pl.when(pl.program_id(0) == 0)
    def _():
        cut_window(own.at[0], halo, row_off[slot], col_off[slot], window)
        power[...] = jnp.zeros(power.shape, F32)

    for rows in BLOCKS:
        real, imag = right_inverse(moved[0, 0, rows, :], moved[0, 1, rows, :], tables, lane)
        before[0, 0, rows, :] = real
        before[0, 1, rows, :] = imag
        real, imag = times(real, imag, window[0, rows, :], window[1, rows, :])
        real, imag = right_forward(real, imag, tables, lane)
        mid[0, rows, :] = real
        mid[1, rows, :] = imag
    for cols in BLOCKS:
        real, imag = left_forward(mid[0, :, cols], mid[1, :, cols], tables, row_table)
        far[0, 0, :, cols] = real
        far[0, 1, :, cols] = imag
        power[:, cols] += real * real + imag * imag


def third_kernel(place, row_off, col_off, counts, far, before, window0, window1, probes, prop,
                 power, power_other, measured, tables, lane, row_table,
                 pieces, keep, send, weight, mid, late, terms):
    slot, core = place[0], place[2]

    @pl.when(pl.program_id(0) == 0)
    def _():
        alive = jnp.where(slot < counts[0], 1.0 / MODES, 0.0).astype(F32)
        weight[...] = (power[...] + power_other[...] - measured[...]) * alive
        terms[...] = jnp.zeros(terms.shape, F32)

    for cols in BLOCKS:
        scale = weight[:, cols]
        real, imag = left_inverse(
            far[0, 0, :, cols] * scale, far[0, 1, :, cols] * scale, tables, row_table
        )
        mid[0, :, cols] = real
        mid[1, :, cols] = imag
    for rows in BLOCKS:
        real, imag = right_inverse(mid[0, rows, :], mid[1, rows, :], tables, lane)
        tr, ti = times_conj(before[0, 0, rows, :], before[0, 1, rows, :], real, imag)
        terms[1, 0, rows, :] += tr
        terms[1, 1, rows, :] += ti
        real, imag = times_conj(window1[0, rows, :], window1[1, rows, :], real, imag)
        real, imag = right_forward(real, imag, tables, lane)
        late[0, rows, :] = real
        late[1, rows, :] = imag
    for cols in BLOCKS:
        real, imag = left_forward(late[0, :, cols], late[1, :, cols], tables, row_table)
        real, imag = times_conj(prop[0, :, cols], prop[1, :, cols], real, imag)
        real, imag = left_inverse(real, imag, tables, row_table)
        mid[0, :, cols] = real
        mid[1, :, cols] = imag
    for index, rows in enumerate(BLOCKS):
        real, imag = right_inverse(mid[0, rows, :], mid[1, rows, :], tables, lane)
        tr, ti = times_conj(probes[0, 0, rows, :], probes[0, 1, rows, :], real, imag)
        terms[0, 0, rows, :] += tr
        terms[0, 1, rows, :] += ti
        pair = times_conj(window0[0, rows, :], window0[1, rows, :], real, imag)
        for part in range(2):
            for group in range(4):
                upper = pair[part][group * 32 : group * 32 + 16]
                lower = pair[part][group * 32 + 16 : group * 32 + 32]
                keep[index * 4 + group, 0, part] = jnp.where(core == 0, upper, lower)
                send[index * 4 + group, 0, part] = jnp.where(core == 0, lower, upper)

    @pl.when(pl.program_id(0) == 3)
    def _():
        for layer in range(2):
            for part in range(2):
                ring = pltpu.roll(terms[layer, part], row_off[slot], 0)
                ring = pltpu.roll(ring, col_off[slot], 1)
                for shard in range(8):
                    pieces[shard, layer, part] = ring[shard * 32 : shard * 32 + 32]


def gather_kernel(place, row_off, col_off, arrived, own, halo):
    shard = place[0] * 2 + place[1]
    rows = lax.broadcasted_iota(jnp.int32, (32, WIN), 0) + shard * 32
    lanes = lax.broadcasted_iota(jnp.int32, (32, HALF), 1)
    for layer in range(2):
        for part in range(2):
            mine = [jnp.zeros((32, HALF), F32) for _ in range(3)]
            next_one = [jnp.zeros((32, HALF), F32) for _ in range(3)]
            for slot in range(4):
                value = arrived[2 * slot, layer, part] + arrived[2 * slot + 1, layer, part]
                inside = rows >= row_off[slot]
                turned = lanes < col_off[slot]
                for store, kept in (
                    (mine, jnp.where(inside, value, 0.0)),
                    (next_one, jnp.where(inside, 0.0, value)),
                ):
                    first, second = kept[:, :HALF], kept[:, HALF:]
                    store[0] = store[0] + jnp.where(turned, 0.0, first)
                    store[1] = store[1] + second
                    store[2] = store[2] + jnp.where(turned, first, 0.0)
            own[layer, part] = jnp.concatenate(mine, axis=1)
            halo[layer, part] = jnp.concatenate(next_one, axis=1)


def join_kernel(first, last, place, *refs):
    out, sem = refs[-2], refs[-1]
    shard = place[0] * 2 + place[1]
    copies = []
    for step in range(first, last):
        start = pl.multiple_of(lax.rem(shard - step + 8, 8) * 32, 32)
        copies.append(
            pltpu.make_async_copy(
                refs[step - first], out.at[:, :, pl.ds(start, 32), :], sem.at[step]
            )
        )
    for copy in copies:
        copy.start()
    for copy in copies:
        copy.wait()


def whole(*sizes):
    return pl.BlockSpec(sizes, lambda *_: (0,) * len(sizes))


def by_mode(*sizes):
    return pl.BlockSpec((1,) + sizes, lambda i, *_: (i,) + (0,) * len(sizes))


def by_home():
    return pl.BlockSpec(
        (8, 1, 2, 16, WIN), lambda i, place, *_: (0, lax.rem(place[0] - i + 4, 4), 0, 0, 0)
    )


TABLES = [whole(4, WIN, WIN), whole(2, 8, HALF), whole(2, HALF, HALF)]
PLANE = whole(WIN, WIN)
FIELD = whole(2, WIN, WIN)
MODAL = by_mode(2, WIN, WIN)
STRIP = whole(2, WIN, COLS)


def layer_of(layer):
    return pl.BlockSpec((1, 2, WIN, COLS), lambda *_: (layer, 0, 0, 0))


ANY = pl.BlockSpec(memory_space=pl.ANY)


def modal_call(body, scalars, steps, ins, outs, out_shape, scratch, aliases=None):
    return pl.pallas_call(
        body,
        out_shape=out_shape,
        grid_spec=pltpu.PrefetchScalarGridSpec(
            num_scalar_prefetch=scalars,
            grid=(steps,),
            in_specs=ins,
            out_specs=outs,
            scratch_shapes=scratch,
        ),
        input_output_aliases=aliases or {},
        compiler_params=PARAMS,
    )


def shape(*sizes):
    return jax.ShapeDtypeStruct(sizes, F32)


def ring_route(size, step):
    return [(i, (i + step) % size) for i in range(size)]


def per_device(object_field, probe, measured, prop_phase, counts, row_offset, col_offset):
    matrices, lane_table, row_table, picks = (jnp.asarray(t) for t in make_tables())
    slot, high, core = lax.axis_index("y"), lax.axis_index("zh"), lax.axis_index("core")
    place = jnp.stack([slot, high, core]).astype(jnp.int32)
    back = [(i, i - 1) for i in range(1, 16)]
    ahead = [(i, i + 1) for i in range(15)]

    halo0 = lax.ppermute(object_field[0], TILE, back)
    half = lax.dynamic_slice_in_dim(probe[0], core * HALF, HALF, axis=1)
    gathered = []
    for k in (1, 2, 3):
        gathered.append(lax.ppermute(half, "y", ring_route(4, k)))
    later, half = lax.optimization_barrier((object_field, half))
    halo1 = lax.ppermute(later[1], TILE, back)
    swap = [(0, 1), (1, 0)]
    mine13 = jnp.stack([gathered[0], gathered[2]])
    mine2 = gathered[1][None]
    other13 = lax.ppermute(mine13, "core", swap)
    other2 = lax.ppermute(mine2, "core", swap)

    wave = jnp.stack([jnp.cos(prop_phase), jnp.sin(prop_phase)])
    prop, target = pl.pallas_call(
        prepare_kernel,
        out_shape=(shape(2, WIN, WIN), shape(WIN, WIN)),
        grid_spec=pltpu.PrefetchScalarGridSpec(
            num_scalar_prefetch=1,
            grid=(1,),
            in_specs=[
                pl.BlockSpec((1, WIN, WIN), lambda i, p: (p[0], 0, 0)), FIELD, FIELD
            ],
            out_specs=[FIELD, PLANE],
        ),
        compiler_params=PARAMS,
        name="prepare",
    )(place, measured, wave, picks)

    modes = shape(4, 2, WIN, WIN)
    tables = (matrices, lane_table, row_table)
    work = [pltpu.VMEM((2, WIN, WIN), F32)]
    moved, probes, window0 = modal_call(
        start_kernel, 3, 1,
        [layer_of(0), STRIP, MODAL, FIELD] + TABLES,
        [MODAL, MODAL, FIELD], (modes, modes, shape(2, WIN, WIN)), work,
    )(place, row_offset, col_offset, object_field, halo0, probe, prop, *tables)
    for base, mine, other in ((1, mine13, other13), (2, mine2, other2)):
        target_block = pl.BlockSpec(
            (1, 2, WIN, WIN), lambda i, *_, base=base: (base + 2 * i, 0, 0, 0)
        )
        moved, probes = modal_call(
            first_kernel, 1, mine.shape[0],
            [FIELD, by_mode(2, HALF, WIN), by_mode(2, HALF, WIN), FIELD] + TABLES + [ANY, ANY],
            [target_block, target_block], (modes, modes), work, {8: 0, 9: 1},
        )(place, window0, mine, other, prop, *tables, moved, probes)

    before, far, power, window1 = modal_call(
        second_kernel, 3, 4,
        [layer_of(1), STRIP, MODAL] + TABLES,
        [MODAL, MODAL, PLANE, FIELD],
        (modes, modes, shape(WIN, WIN), shape(2, WIN, WIN)),
        work,
    )(place, row_offset, col_offset, object_field, halo1, moved, *tables)

    power_other = lax.ppermute(power, "zh", [(0, 1), (1, 0)])

    parts_shape = shape(8, 4, 2, 16, WIN)
    pieces, keep, send = modal_call(
        third_kernel, 4, 4,
        [MODAL, MODAL, FIELD, FIELD, MODAL, FIELD, PLANE, PLANE, PLANE] + TABLES,
        [whole(8, 2, 2, 32, WIN), by_home(), by_home()],
        (shape(8, 2, 2, 32, WIN), parts_shape, parts_shape),
        [
            pltpu.VMEM((WIN, WIN), F32),
            pltpu.VMEM((2, WIN, WIN), F32),
            pltpu.VMEM((2, WIN, WIN), F32),
            pltpu.VMEM((2, 2, WIN, WIN), F32),
        ],
    )(place, row_offset, col_offset, counts, far, before, window0, window1, probes, prop, power,
      power_other, target, *tables)

    swapped = lax.ppermute(send, "core", [(0, 1), (1, 0)])
    arrived = lax.all_to_all(pieces, MODE, 0, 0)
    own, over = pl.pallas_call(
        gather_kernel,
        out_shape=(shape(2, 2, 32, COLS), shape(2, 2, 32, COLS)),
        in_specs=[SMEM] * 3 + [VMEM],
        out_specs=[VMEM] * 2,
        compiler_params=PARAMS,
        name="gather",
    )(place, row_offset, col_offset, arrived)
    over_in = lax.ppermute(over, TILE, ahead)
    spread = lax.all_to_all((keep + swapped).reshape(32, 2, 16, WIN), SPREAD, 0, 0)
    probe_part = jnp.sum(spread, axis=0)

    total = own + over_in
    parts = []
    for k in range(1, 8):
        parts.append(lax.ppermute(total, MODE, ring_route(8, k)))
    probe_all = lax.all_to_all(jnp.broadcast_to(probe_part, (16, 2, 16, WIN)), TILE, 0, 0)
    object_grad = pl.pallas_call(
        functools.partial(join_kernel, 0, 1),
        out_shape=shape(2, 2, WIN, COLS),
        in_specs=[SMEM, VMEM],
        out_specs=ANY,
        scratch_shapes=[pltpu.SemaphoreType.DMA((8,))],
        compiler_params=PARAMS,
        name="joina",
    )(place, total)
    object_grad = pl.pallas_call(
        functools.partial(join_kernel, 1, 8),
        out_shape=shape(2, 2, WIN, COLS),
        in_specs=[SMEM] + [VMEM] * 7 + [ANY],
        out_specs=ANY,
        scratch_shapes=[pltpu.SemaphoreType.DMA((8,))],
        input_output_aliases={8: 0},
        compiler_params=PARAMS,
        name="joinb",
    )(place, *parts, object_grad)
    probe_grad = jnp.transpose(probe_all, (1, 0, 2, 3)).reshape(1, 2, WIN, WIN)
    return object_grad, probe_grad


def solution(mesh):
    fine = Mesh(mesh.devices.reshape(2, 4, 2, 4, 2), ("zl", "x", "core", "y", "zh"))
    placed = (
        P(None, None, TILE, None),
        P(MODE, None, None, None),
        P(TILE, None, None),
        P(),
        P(TILE),
        P(TILE),
        P(TILE),
    )

    return jax.shard_map(
        per_device,
        mesh=fine,
        in_specs=placed,
        out_specs=(P(None, None, TILE, None), P(MODE, None, None, None)),
        check_vma=False,
    )
```

profile of v0, /device:TPU:0, one launch (start us, length us, event | category | flops | bytes accessed | tf_op | source)
XLA Modules:
  0.0 156.1 jit_solution(15823838461354914460)
XLA Ops:
  0.6 0.0 copy-start
  0.6 1.1 dynamic-slice_bitcast_fusion
  1.7 0.0 copy-start.12
  1.8 3.2 %collective-permute-start.5 = (f32[2,128,256]{2,1,0:T(8,128)S(1)}, f32[2,128,256]{2,1,0:T(8,128)S(1)}, u32[]{:S(2)}, u32[]{:S(2)}) collective-permute-start(f32[2,128,256]{2,1,0:T(8,128)S(1)} %dynamic-slice_bitcast_fusion), channel_id=1, source_target_pairs={{0,6},{2,0},{4,2},{6,4},{1,7},{3,1},{5,3},{7,5},{8,14},{10,8},{12,... | collective-permute-start | bytes 786440 | tf_op jit(solution)/shard_map/ppermute | solution.py:389
  4.9 0.0 collective-permute-start.4
  5.0 2.1 %slice_bitcast_fusion = f32[2,256,384]{2,1,0:T(8,128)} fusion(f32[2,2,256,384]{3,2,1,0:T(8,128)} %own.3), kind=kLoop, calls=%fused_computation | loop fusion | bytes 1572864 | tf_op jit(solution)/shard_map/squeeze | solution.py:385
  7.0 1.3 collective-permute-start.1
  8.3 0.9 slice_bitcast_fusion.1
  9.3 1.3 collective-permute-start
  10.5 2.3 %collective-permute-start.2 = (f32[2,128,256]{2,1,0:T(8,128)S(1)}, f32[2,128,256]{2,1,0:T(8,128)S(1)}, u32[]{:S(2)}, u32[]{:S(2)}) collective-permute-start(f32[2,128,256]{2,1,0:T(8,128)S(1)} %dynamic-slice_bitcast_fusion), channel_id=1, source_target_pairs={{0,4},{2,6},{4,0},{6,2},{1,5},{3,7},{5,1},{7,3},{8,12},{10,14},{12... | collective-permute-start | bytes 786440 | tf_op jit(solution)/shard_map/ppermute | solution.py:389
  12.8 0.0 collective-permute-done.5
  12.8 1.1 collective-permute-done.4
  14.0 0.0 copy-start.1
  14.0 0.0 copy-start.2
  14.0 0.0 copy-start.3
  14.0 0.0 copy-start.7
  14.0 0.0 copy-start.8
  14.0 0.5 collective-permute-start.6
  14.5 6.0 %collective-permute-done.2 = f32[2,128,256]{2,1,0:T(8,128)S(1)} collective-permute-done((f32[2,128,256]{2,1,0:T(8,128)S(1)}, f32[2,128,256]{2,1,0:T(8,128)S(1)}, u32[]{:S(2)}, u32[]{:S(2)}) %collective-permute-start.2) | collective-permute-done | bytes 262176 | tf_op jit(solution)/shard_map/ppermute | solution.py:389
  20.5 0.6 collective-permute-start.3
  21.1 1.6 %cosine_bitcast_fusion = (f32[1,256,256]{2,1,0:T(8,128)}, f32[1,256,256]{2,1,0:T(8,128)}) fusion(f32[256,256]{1,0:T(8,128)S(1)} %copy-done.12), kind=kLoop, calls=%fused_computation.5 | loop fusion | bytes 786432 | tf_op jit(solution)/shard_map/stack | solution.py:398
  22.8 0.1 pad_add_fusion.place
  22.8 1.1 pad_maximum_fusion.wave
  23.9 0.0 copy-start.4
  23.9 1.2 copy-done.4
  25.1 0.9 copy-done.6
  26.1 1.6 %prepare.1 = (f32[2,256,256]{2,1,0:T(8,128)S(1)}, f32[256,256]{1,0:T(8,128)S(1)}) custom-call(s32[3]{0:T(128)S(1)} %pad_add_fusion.place, f32[4,256,256]{2,1,0:T(8,128)S(1)} %copy-done.4, f32[2,256,256]{2,1,0:T(8,128)S(1)} %pad_maximum_fusion.wave, bf16[2,256,256]{2,1,0:T(8,128)(2,1)S(1)} %copy-done.6), custom_call_target="tpu_custom_call" | custom-call | tf_op jit(solution)/shard_map/prepare/pallas_call | solution.py:399
  27.7 0.0 collective-permute-done.1.halo
  27.7 0.0 copy-start.9
  27.7 0.6 copy-done.9
  28.4 3.4 %shard_map.122 = (f32[4,2,256,256]{3,2,1,0:T(8,128)S(1)}, f32[4,2,256,256]{3,2,1,0:T(8,128)S(1)}, f32[2,256,256]{2,1,0:T(8,128)S(1)}) custom-call(s32[3]{0:T(128)S(1)} %pad_add_fusion.place, s32[4]{0:T(128)S(1)} %copy-done.8, s32[4]{0:T(128)S(1)} %copy-done.9, f32[2,2,256,384]{3,2,1,0:T(8,128)S(1)} %copy-done, f32[2,256,384]{2,1,0:T(8,128)} %collective-permute-done.1.halo, ...), custom_call_target="tpu_custom_call" | custom-call | tf_op jit(solution)/shard_map/pallas_call | solution.py:417
  31.8 0.0 collective-permute-done.6.other
  31.8 4.1 %shard_map.123 = (f32[4,2,256,256]{3,2,1,0:T(8,128)S(1)}, f32[4,2,256,256]{3,2,1,0:T(8,128)S(1)}) custom-call(s32[3]{0:T(128)S(1)} %pad_add_fusion.place, f32[2,256,256]{2,1,0:T(8,128)S(1)} %get-tuple-element.23.window.window0, f32[2,2,128,256]{3,2,1,0:T(8,128)S(1)} %pad_maximum_fusion.1.mine, ...), custom_call_target="tpu_custom_call", output_to_operand_aliasing={{0}: (8, {}), {1}: (9, {})} | custom-call | tf_op jit(solution)/shard_map/pallas_call | solution.py:426
  36.0 0.0 copy-start.10
  36.0 2.8 %shard_map.124 = (f32[4,2,256,256]{3,2,1,0:T(8,128)S(1)}, f32[4,2,256,256]{3,2,1,0:T(8,128)S(1)}) custom-call(s32[3]{0:T(128)S(1)} %pad_add_fusion.place, f32[2,256,256]{2,1,0:T(8,128)S(1)} %get-tuple-element.23.window.window0, f32[1,2,128,256]{3,2,1,0:T(8,128)S(1)} %bitcast.21, ...), custom_call_target="tpu_custom_call", output_to_operand_aliasing={{0}: (8, {}), {1}: (9, {})} | custom-call | tf_op jit(solution)/shard_map/pallas_call | solution.py:426
  38.8 7.4 %shard_map.125 = (f32[4,2,256,256]{3,2,1,0:T(8,128)S(1)}, f32[4,2,256,256]{3,2,1,0:T(8,128)S(1)}, f32[256,256]{1,0:T(8,128)S(1)}, f32[2,256,256]{2,1,0:T(8,128)S(1)}) custom-call(s32[3]{0:T(128)S(1)} %pad_add_fusion.place, s32[4]{0:T(128)S(1)} %copy-done.8, s32[4]{0:T(128)S(1)} %copy-done.10, f32[2,2,256,384]{3,2,1,0:T(8,128)S(1)} %copy-done, ...), custom_call_target="tpu_custom_call" | custom-call | tf_op jit(solution)/shard_map/pallas_call | solution.py:432
  46.2 4.0 %collective-permute-start.7 = (f32[256,256]{1,0:T(8,128)S(1)}, f32[256,256]{1,0:T(8,128)S(1)}, u32[]{:S(2)}, u32[]{:S(2)}) collective-permute-start(f32[256,256]{1,0:T(8,128)S(1)} %get-tuple-element.33.power), channel_id=1, source_target_pairs={{0,1},{1,0},{2,3},{3,2},{4,5},{5,4},{6,7},{7,6},{8,9},{9,8},{10,11... | collective-permute-start | bytes 786440 | tf_op jit(solution)/shard_map/ppermute | solution.py:440
  50.8 5.8 %collective-permute-done.7.power_other = f32[256,256]{1,0:T(8,128)S(1)} collective-permute-done((f32[256,256]{1,0:T(8,128)S(1)}, f32[256,256]{1,0:T(8,128)S(1)}, u32[]{:S(2)}, u32[]{:S(2)}) %collective-permute-start.7) | collective-permute-done | bytes 262176 | tf_op jit(solution)/shard_map/ppermute | solution.py:440
  56.7 12.5 %shard_map.126 = (f32[8,2,2,32,256]{4,3,2,1,0:T(8,128)S(1)}, f32[8,4,2,16,256]{4,3,2,1,0:T(8,128)S(1)}, f32[8,4,2,16,256]{4,3,2,1,0:T(8,128)}) custom-call(s32[3]{0:T(128)S(1)} %pad_add_fusion.place, s32[4]{0:T(128)S(1)} %copy-done.8, s32[4]{0:T(128)S(1)} %copy-done.10, s32[1]{0:T(128)S(6)} %copy.24.counts, f32[4,2,256,256]{3,2,1,0:T(8,128)S(1)} %get-tuple-element.29.far, ...), custom_call_target="tpu_custom_call" | custom-call | tf_op jit(solution)/shard_map/pallas_call | solution.py:443
  69.2 1.0 copy-done.5
  70.2 7.2 %all-to-all-start = ((f32[8,2,2,32,256]{4,3,2,1,0:T(8,128)}), f32[8,2,2,32,256]{4,3,2,1,0:T(8,128)S(1)}, u32[]{:S(2)}, u32[]{:S(2)}) async-start(f32[8,2,2,32,256]{4,3,2,1,0:T(8,128)} %copy-done.5), calls=%async_computation | async-start | bytes 2097152 | tf_op jit(solution)/shard_map/all_to_all | solution.py:458
  77.4 0.0 copy-start.11
  77.4 1.2 add.11
  78.6 16.1 %all-to-all-done.arrived = f32[8,2,2,32,256]{4,3,2,1,0:T(8,128)S(1)} async-done(((f32[8,2,2,32,256]{4,3,2,1,0:T(8,128)}), f32[8,2,2,32,256]{4,3,2,1,0:T(8,128)S(1)}, u32[]{:S(2)}, u32[]{:S(2)}) %all-to-all-start) | async-done | bytes 1048608 | tf_op jit(solution)/shard_map/all_to_all | solution.py:458
  94.7 8.6 %all-to-all-start.1 = ((f32[32,2,16,256]{3,2,1,0:T(8,128)}), f32[32,2,16,256]{3,2,1,0:T(8,128)S(1)}, u32[]{:S(2)}, u32[]{:S(2)}) async-start(f32[32,2,16,256]{3,2,1,0:T(8,128)} %bitcast.11), calls=%async_computation.1 | async-start | bytes 2097152 | tf_op jit(solution)/shard_map/all_to_all | solution.py:468
  103.4 0.7 gather.1
  104.1 1.7 %collective-permute-start.8 = (f32[2,2,32,384]{3,2,1,0:T(8,128)S(1)}, f32[2,2,32,384]{3,2,1,0:T(8,128)S(1)}, u32[]{:S(2)}, u32[]{:S(2)}) collective-permute-start(f32[2,2,32,384]{3,2,1,0:T(8,128)S(1)} %get-tuple-element.37), channel_id=1, source_target_pairs={{0,8},{8,16},{16,24},{24,32},{32,40},{40,48},{48,56},{56,64},{64,7... | collective-permute-start | bytes 589832 | tf_op jit(solution)/shard_map/ppermute | solution.py:467
  105.8 15.2 %all-to-all-done.1 = f32[32,2,16,256]{3,2,1,0:T(8,128)S(1)} async-done(((f32[32,2,16,256]{3,2,1,0:T(8,128)}), f32[32,2,16,256]{3,2,1,0:T(8,128)S(1)}, u32[]{:S(2)}, u32[]{:S(2)}) %all-to-all-start.1) | async-done | bytes 1048608 | tf_op jit(solution)/shard_map/all_to_all | solution.py:468
  120.9 0.1 reduce_sum.9
  121.0 0.9 broadcast_in_dim.7
  121.9 3.6 %all-to-all-start.2 = ((f32[16,2,16,256]{3,2,1,0:T(8,128)}), f32[16,2,16,256]{3,2,1,0:T(8,128)S(1)}, u32[]{:S(2)}, u32[]{:S(2)}) async-start(f32[16,2,16,256]{3,2,1,0:T(8,128)} %broadcast_in_dim.7), calls=%async_computation.2 | async-start | bytes 1048576 | tf_op jit(solution)/shard_map/all_to_all | solution.py:475
  125.5 0.4 collective-permute-start.10
  125.9 2.1 %collective-permute-start.11 = (f32[2,2,32,384]{3,2,1,0:T(8,128)S(1)}, f32[2,2,32,384]{3,2,1,0:T(8,128)S(1)}, u32[]{:S(2)}, u32[]{:S(2)}) collective-permute-start(f32[2,2,32,384]{3,2,1,0:T(8,128)S(1)} %add.10.refs_0_), channel_id=1, source_target_pairs={{0,3},{1,4},{2,5},{3,6},{4,7},{5,0},{6,1},{7,2},{8,11},{9,12},{10,... | collective-permute-start | bytes 589832 | tf_op jit(solution)/shard_map/ppermute | solution.py:474
  128.1 3.2 %collective-permute-start.12 = (f32[2,2,32,384]{3,2,1,0:T(8,128)S(1)}, f32[2,2,32,384]{3,2,1,0:T(8,128)S(1)}, u32[]{:S(2)}, u32[]{:S(2)}) collective-permute-start(f32[2,2,32,384]{3,2,1,0:T(8,128)S(1)} %add.10.refs_0_), channel_id=1, source_target_pairs={{0,4},{1,5},{2,6},{3,7},{4,0},{5,1},{6,2},{7,3},{8,12},{9,13},{10,... | collective-permute-start | bytes 589832 | tf_op jit(solution)/shard_map/ppermute | solution.py:474
  131.3 2.5 %collective-permute-start.13 = (f32[2,2,32,384]{3,2,1,0:T(8,128)S(1)}, f32[2,2,32,384]{3,2,1,0:T(8,128)S(1)}, u32[]{:S(2)}, u32[]{:S(2)}) collective-permute-start(f32[2,2,32,384]{3,2,1,0:T(8,128)S(1)} %add.10.refs_0_), channel_id=1, source_target_pairs={{0,5},{1,6},{2,7},{3,0},{4,1},{5,2},{6,3},{7,4},{8,13},{9,14},{10,... | collective-permute-start | bytes 589832 | tf_op jit(solution)/shard_map/ppermute | solution.py:474
  133.8 1.8 %collective-permute-start.14 = (f32[2,2,32,384]{3,2,1,0:T(8,128)S(1)}, f32[2,2,32,384]{3,2,1,0:T(8,128)S(1)}, u32[]{:S(2)}, u32[]{:S(2)}) collective-permute-start(f32[2,2,32,384]{3,2,1,0:T(8,128)S(1)} %add.10.refs_0_), channel_id=1, source_target_pairs={{0,6},{1,7},{2,0},{3,1},{4,2},{5,3},{6,4},{7,5},{8,14},{9,15},{10,... | collective-permute-start | bytes 589832 | tf_op jit(solution)/shard_map/ppermute | solution.py:474
  135.6 7.3 %collective-permute-start.15 = (f32[2,2,32,384]{3,2,1,0:T(8,128)S(1)}, f32[2,2,32,384]{3,2,1,0:T(8,128)S(1)}, u32[]{:S(2)}, u32[]{:S(2)}) collective-permute-start(f32[2,2,32,384]{3,2,1,0:T(8,128)S(1)} %add.10.refs_0_), channel_id=1, source_target_pairs={{0,7},{1,0},{2,1},{3,2},{4,3},{5,4},{6,5},{7,6},{8,15},{9,8},{10,9... | collective-permute-start | bytes 589832 | tf_op jit(solution)/shard_map/ppermute | solution.py:474
  142.9 1.0 collective-permute-start.9
  143.9 1.3 joina.1.refs_7_
  145.2 2.7 %collective-permute-done.13.refs_4_ = f32[2,2,32,384]{3,2,1,0:T(8,128)S(1)} collective-permute-done((f32[2,2,32,384]{3,2,1,0:T(8,128)S(1)}, f32[2,2,32,384]{3,2,1,0:T(8,128)S(1)}, u32[]{:S(2)}, u32[]{:S(2)}) %collective-permute-start.13) | collective-permute-done | bytes 196640 | tf_op jit(solution)/shard_map/ppermute | solution.py:474
  147.9 2.1 %collective-permute-done.15.refs_6_ = f32[2,2,32,384]{3,2,1,0:T(8,128)S(1)} collective-permute-done((f32[2,2,32,384]{3,2,1,0:T(8,128)S(1)}, f32[2,2,32,384]{3,2,1,0:T(8,128)S(1)}, u32[]{:S(2)}, u32[]{:S(2)}) %collective-permute-start.15) | collective-permute-done | bytes 196640 | tf_op jit(solution)/shard_map/ppermute | solution.py:474
  150.0 3.5 %collective-permute-done.9.refs_0_ = f32[2,2,32,384]{3,2,1,0:T(8,128)S(1)} collective-permute-done((f32[2,2,32,384]{3,2,1,0:T(8,128)S(1)}, f32[2,2,32,384]{3,2,1,0:T(8,128)S(1)}, u32[]{:S(2)}, u32[]{:S(2)}) %collective-permute-start.9) | collective-permute-done | bytes 196640 | tf_op jit(solution)/shard_map/ppermute | solution.py:474
  153.6 1.7 %joinb.1 = f32[2,2,256,384]{3,2,1,0:T(8,128)} custom-call(s32[3]{0:T(128)S(1)} %pad_add_fusion.place, f32[2,2,32,384]{3,2,1,0:T(8,128)S(1)} %collective-permute-done.9.refs_0_, f32[2,2,32,384]{3,2,1,0:T(8,128)S(1)} %collective-permute-done.10.refs_1_, f32[2,2,32,384]{3,2,1,0:T(8,128)S(1)} %collective-permute-done.11.refs_2_, ...), custom_call_target="tpu_custom_call", output_to_operand_aliasing={{}: (8, {})} | custom-call | tf_op jit(solution)/shard_map/joinb/pallas_call | solution.py:485
  155.3 0.8 copy.18
  (23 shorter events, 0.1 us)
Async XLA Ops:
  0.6 7.7 %copy-start = (f32[2,2,256,384]{3,2,1,0:T(8,128)S(1)}, f32[2,2,256,384]{3,2,1,0:T(8,128)}, u32[]{:S(2)}) copy-start(f32[2,2,256,384]{3,2,1,0:T(8,128)} %own.3) | copy-start | bytes 4718596
  1.7 19.4 %copy-start.12 = (f32[256,256]{1,0:T(8,128)S(1)}, f32[256,256]{1,0:T(8,128)}, u32[]{:S(2)}) copy-start(f32[256,256]{1,0:T(8,128)} %param.14) | copy-start | bytes 786436
  1.8 11.1 %collective-permute-start.5 = (f32[2,128,256]{2,1,0:T(8,128)S(1)}, f32[2,128,256]{2,1,0:T(8,128)S(1)}, u32[]{:S(2)}, u32[]{:S(2)}) collective-permute-start(f32[2,128,256]{2,1,0:T(8,128)S(1)} %dynamic-slice_bitcast_fusion), channel_id=1, source_target_pairs={{0,6},{2,0},{4,2},{6,4},{1,7},{3,1},{5,3},{7,5},{8,14},{10,8},{12,... | collective-permute-start | bytes 786440 | tf_op jit(solution)/shard_map/ppermute | solution.py:389
  4.9 9.0 %collective-permute-start.4 = (f32[2,128,256]{2,1,0:T(8,128)S(1)}, f32[2,128,256]{2,1,0:T(8,128)S(1)}, u32[]{:S(2)}, u32[]{:S(2)}) collective-permute-start(f32[2,128,256]{2,1,0:T(8,128)S(1)} %dynamic-slice_bitcast_fusion), channel_id=1, source_target_pairs={{0,2},{2,4},{4,6},{6,0},{1,3},{3,5},{5,7},{7,1},{8,10},{10,12},{12... | collective-permute-start | bytes 786440 | tf_op jit(solution)/shard_map/ppermute | solution.py:389
  7.0 20.6 %collective-permute-start.1 = (f32[2,256,384]{2,1,0:T(8,128)}, f32[2,256,384]{2,1,0:T(8,128)}, u32[]{:S(2)}, u32[]{:S(2)}) collective-permute-start(f32[2,256,384]{2,1,0:T(8,128)} %slice_bitcast_fusion), channel_id=1, source_target_pairs={{8,0},{16,8},{24,16},{32,24},{40,32},{48,40},{56,48},{64,56},{72,6... | collective-permute-start | bytes 2359304 | tf_op jit(solution)/shard_map/ppermute | solution.py:385
  9.3 29.6 %collective-permute-start = (f32[2,256,384]{2,1,0:T(8,128)}, f32[2,256,384]{2,1,0:T(8,128)}, u32[]{:S(2)}, u32[]{:S(2)}) collective-permute-start(f32[2,256,384]{2,1,0:T(8,128)} %slice_bitcast_fusion.1), channel_id=1, source_target_pairs={{8,0},{16,8},{24,16},{32,24},{40,32},{48,40},{56,48},{64,56},{72,6... | collective-permute-start | bytes 2359304 | tf_op jit(solution)/shard_map/ppermute | solution.py:391
  10.5 10.0 %collective-permute-start.2 = (f32[2,128,256]{2,1,0:T(8,128)S(1)}, f32[2,128,256]{2,1,0:T(8,128)S(1)}, u32[]{:S(2)}, u32[]{:S(2)}) collective-permute-start(f32[2,128,256]{2,1,0:T(8,128)S(1)} %dynamic-slice_bitcast_fusion), channel_id=1, source_target_pairs={{0,4},{2,6},{4,0},{6,2},{1,5},{3,7},{5,1},{7,3},{8,12},{10,14},{12... | collective-permute-start | bytes 786440 | tf_op jit(solution)/shard_map/ppermute | solution.py:389
  14.0 13.7 %copy-start.1 = (bf16[4,256,256]{2,1,0:T(8,128)(2,1)S(1)}, bf16[4,256,256]{2,1,0:T(8,128)(2,1)}, u32[]{:S(2)}) copy-start(bf16[4,256,256]{2,1,0:T(8,128)(2,1)} %constant.28.clone.tables) | copy-start | bytes 1572868
  14.0 13.7 %copy-start.2 = (f32[2,128,128]{2,1,0:T(8,128)S(1)}, f32[2,128,128]{2,1,0:T(8,128)}, u32[]{:S(2)}) copy-start(f32[2,128,128]{2,1,0:T(8,128)} %constant.30.clone.row_table) | copy-start | bytes 393220
  14.0 13.7 %copy-start.3 = (f32[1,2,256,256]{3,2,1,0:T(8,128)S(1)}, f32[1,2,256,256]{3,2,1,0:T(8,128)}, u32[]{:S(2)}) copy-start(f32[1,2,256,256]{3,2,1,0:T(8,128)} %probe.1) | copy-start | bytes 1572868
  14.0 13.7 %copy-start.7 = (f32[2,8,128]{2,1,0:T(8,128)S(1)}, f32[2,8,128]{2,1,0:T(8,128)}, u32[]{:S(2)}) copy-start(f32[2,8,128]{2,1,0:T(8,128)} %constant.29.clone.lane) | copy-start | bytes 24580
  14.0 13.7 %copy-start.8 = (s32[4]{0:T(128)S(1)}, s32[4]{0:T(128)}, u32[]{:S(2)}) copy-start(s32[4]{0:T(128)} %row_off.7) | copy-start | bytes 52
  14.0 17.8 %collective-permute-start.6 = (f32[2,2,128,256]{3,2,1,0:T(8,128)S(1)}, f32[2,2,128,256]{3,2,1,0:T(8,128)}, u32[]{:S(2)}, u32[]{:S(2)}) collective-permute-start(f32[2,2,128,256]{3,2,1,0:T(8,128)S(1)} %pad_maximum_fusion.1.mine), channel_id=1, source_target_pairs={{0,8},{8,0},{1,9},{9,1},{2,10},{10,2},{3,11},{11,3},{4,12},{12,4},... | collective-permute-start | bytes 1572872 | tf_op jit(solution)/shard_map/ppermute | solution.py:395
  20.5 15.5 %collective-permute-start.3 = (f32[1,2,128,256]{3,2,1,0:T(8,128)S(1)}, f32[1,2,128,256]{3,2,1,0:T(8,128)}, u32[]{:S(2)}, u32[]{:S(2)}) collective-permute-start(f32[1,2,128,256]{3,2,1,0:T(8,128)S(1)} %bitcast.20), channel_id=1, source_target_pairs={{0,8},{8,0},{1,9},{9,1},{2,10},{10,2},{3,11},{11,3},{4,12},{12,4},... | collective-permute-start | bytes 786440 | tf_op jit(solution)/shard_map/ppermute | solution.py:396
  23.9 1.2 copy-start.4
  25.1 0.9 copy-start.6
  27.7 0.7 copy-start.9
  36.0 2.8 %copy-start.10 = (s32[4]{0:T(128)S(1)}, s32[4]{0:T(128)}, u32[]{:S(2)}) copy-start(s32[4]{0:T(128)} %col_off.7) | copy-start | bytes 52
  46.2 10.5 %collective-permute-start.7 = (f32[256,256]{1,0:T(8,128)S(1)}, f32[256,256]{1,0:T(8,128)S(1)}, u32[]{:S(2)}, u32[]{:S(2)}) collective-permute-start(f32[256,256]{1,0:T(8,128)S(1)} %get-tuple-element.33.power), channel_id=1, source_target_pairs={{0,1},{1,0},{2,3},{3,2},{4,5},{5,4},{6,7},{7,6},{8,9},{9,8},{10,11... | collective-permute-start | bytes 786440 | tf_op jit(solution)/shard_map/ppermute | solution.py:440
  69.2 1.0 copy-start.5
  70.2 7.2 %collective-permute-start.16 = (f32[8,4,2,16,256]{4,3,2,1,0:T(8,128)}, f32[8,4,2,16,256]{4,3,2,1,0:T(8,128)S(1)}, u32[]{:S(2)}, u32[]{:S(2)}) collective-permute-start(f32[8,4,2,16,256]{4,3,2,1,0:T(8,128)} %get-tuple-element.39), channel_id=1, source_target_pairs={{0,8},{8,0},{1,9},{9,1},{2,10},{10,2},{3,11},{11,3},{4,12},{12,4},... | collective-permute-start | bytes 3145736 | tf_op jit(solution)/shard_map/ppermute | solution.py:457
  70.2 24.5 %all-to-all-start = ((f32[8,2,2,32,256]{4,3,2,1,0:T(8,128)}), f32[8,2,2,32,256]{4,3,2,1,0:T(8,128)S(1)}, u32[]{:S(2)}, u32[]{:S(2)}) async-start(f32[8,2,2,32,256]{4,3,2,1,0:T(8,128)} %copy-done.5), calls=%async_computation | async-start | bytes 2097152 | tf_op jit(solution)/shard_map/all_to_all | solution.py:458
  77.4 26.0 %copy-start.11 = (s32[4]{0:T(128)S(1)}, s32[4]{0:T(128)}, u32[]{:S(2)}) copy-start(s32[4]{0:T(128)} %col_off.7) | copy-start | bytes 52
  94.7 26.2 %all-to-all-start.1 = ((f32[32,2,16,256]{3,2,1,0:T(8,128)}), f32[32,2,16,256]{3,2,1,0:T(8,128)S(1)}, u32[]{:S(2)}, u32[]{:S(2)}) async-start(f32[32,2,16,256]{3,2,1,0:T(8,128)} %bitcast.11), calls=%async_computation.1 | async-start | bytes 2097152 | tf_op jit(solution)/shard_map/all_to_all | solution.py:468
  104.1 21.4 %collective-permute-start.8 = (f32[2,2,32,384]{3,2,1,0:T(8,128)S(1)}, f32[2,2,32,384]{3,2,1,0:T(8,128)S(1)}, u32[]{:S(2)}, u32[]{:S(2)}) collective-permute-start(f32[2,2,32,384]{3,2,1,0:T(8,128)S(1)} %get-tuple-element.37), channel_id=1, source_target_pairs={{0,8},{8,16},{16,24},{24,32},{32,40},{40,48},{48,56},{56,64},{64,7... | collective-permute-start | bytes 589832 | tf_op jit(solution)/shard_map/ppermute | solution.py:467
  121.9 33.4 %all-to-all-start.2 = ((f32[16,2,16,256]{3,2,1,0:T(8,128)}), f32[16,2,16,256]{3,2,1,0:T(8,128)S(1)}, u32[]{:S(2)}, u32[]{:S(2)}) async-start(f32[16,2,16,256]{3,2,1,0:T(8,128)} %broadcast_in_dim.7), calls=%async_computation.2 | async-start | bytes 1048576 | tf_op jit(solution)/shard_map/all_to_all | solution.py:475
  125.5 10.1 %collective-permute-start.10 = (f32[2,2,32,384]{3,2,1,0:T(8,128)S(1)}, f32[2,2,32,384]{3,2,1,0:T(8,128)S(1)}, u32[]{:S(2)}, u32[]{:S(2)}) collective-permute-start(f32[2,2,32,384]{3,2,1,0:T(8,128)S(1)} %add.10.refs_0_), channel_id=1, source_target_pairs={{0,2},{1,3},{2,4},{3,5},{4,6},{5,7},{6,0},{7,1},{8,10},{9,11},{10,... | collective-permute-start | bytes 589832 | tf_op jit(solution)/shard_map/ppermute | solution.py:474
  125.9 17.0 %collective-permute-start.11 = (f32[2,2,32,384]{3,2,1,0:T(8,128)S(1)}, f32[2,2,32,384]{3,2,1,0:T(8,128)S(1)}, u32[]{:S(2)}, u32[]{:S(2)}) collective-permute-start(f32[2,2,32,384]{3,2,1,0:T(8,128)S(1)} %add.10.refs_0_), channel_id=1, source_target_pairs={{0,3},{1,4},{2,5},{3,6},{4,7},{5,0},{6,1},{7,2},{8,11},{9,12},{10,... | collective-permute-start | bytes 589832 | tf_op jit(solution)/shard_map/ppermute | solution.py:474
  128.1 17.2 %collective-permute-start.12 = (f32[2,2,32,384]{3,2,1,0:T(8,128)S(1)}, f32[2,2,32,384]{3,2,1,0:T(8,128)S(1)}, u32[]{:S(2)}, u32[]{:S(2)}) collective-permute-start(f32[2,2,32,384]{3,2,1,0:T(8,128)S(1)} %add.10.refs_0_), channel_id=1, source_target_pairs={{0,4},{1,5},{2,6},{3,7},{4,0},{5,1},{6,2},{7,3},{8,12},{9,13},{10,... | collective-permute-start | bytes 589832 | tf_op jit(solution)/shard_map/ppermute | solution.py:474
  131.3 16.6 %collective-permute-start.13 = (f32[2,2,32,384]{3,2,1,0:T(8,128)S(1)}, f32[2,2,32,384]{3,2,1,0:T(8,128)S(1)}, u32[]{:S(2)}, u32[]{:S(2)}) collective-permute-start(f32[2,2,32,384]{3,2,1,0:T(8,128)S(1)} %add.10.refs_0_), channel_id=1, source_target_pairs={{0,5},{1,6},{2,7},{3,0},{4,1},{5,2},{6,3},{7,4},{8,13},{9,14},{10,... | collective-permute-start | bytes 589832 | tf_op jit(solution)/shard_map/ppermute | solution.py:474
  133.8 14.1 %collective-permute-start.14 = (f32[2,2,32,384]{3,2,1,0:T(8,128)S(1)}, f32[2,2,32,384]{3,2,1,0:T(8,128)S(1)}, u32[]{:S(2)}, u32[]{:S(2)}) collective-permute-start(f32[2,2,32,384]{3,2,1,0:T(8,128)S(1)} %add.10.refs_0_), channel_id=1, source_target_pairs={{0,6},{1,7},{2,0},{3,1},{4,2},{5,3},{6,4},{7,5},{8,14},{9,15},{10,... | collective-permute-start | bytes 589832 | tf_op jit(solution)/shard_map/ppermute | solution.py:474
  135.6 14.4 %collective-permute-start.15 = (f32[2,2,32,384]{3,2,1,0:T(8,128)S(1)}, f32[2,2,32,384]{3,2,1,0:T(8,128)S(1)}, u32[]{:S(2)}, u32[]{:S(2)}) collective-permute-start(f32[2,2,32,384]{3,2,1,0:T(8,128)S(1)} %add.10.refs_0_), channel_id=1, source_target_pairs={{0,7},{1,0},{2,1},{3,2},{4,3},{5,4},{6,5},{7,6},{8,15},{9,8},{10,9... | collective-permute-start | bytes 589832 | tf_op jit(solution)/shard_map/ppermute | solution.py:474
  142.9 10.6 %collective-permute-start.9 = (f32[2,2,32,384]{3,2,1,0:T(8,128)S(1)}, f32[2,2,32,384]{3,2,1,0:T(8,128)S(1)}, u32[]{:S(2)}, u32[]{:S(2)}) collective-permute-start(f32[2,2,32,384]{3,2,1,0:T(8,128)S(1)} %add.10.refs_0_), channel_id=1, source_target_pairs={{0,1},{1,2},{2,3},{3,4},{4,5},{5,6},{6,7},{7,0},{8,9},{9,10},{10,1... | collective-permute-start | bytes 589832 | tf_op jit(solution)/shard_map/ppermute | solution.py:474
where the time goes:
time: 159 us; the launch traced here: 156 us
  starting transfers between devices  52.6 us (33%)
  waiting for transfers between devices  52.6 us (33%)
  Pallas kernels  35.5 us (22%)
  local copies, waits for them, and re-layouts  11.3 us (7%)
  other arithmetic  2.46 us (2%)
  between operations  1.63 us (1%)
    ppermute x7, starting transfers between devices, per_device(): parts.append(lax.ppermute(total, MODE, ring_route(8, k)))  18.4 us
    all_to_all x1, waiting for transfers between devices, per_device(): arrived = lax.all_to_all(pieces, MODE, 0, 0)  16.1 us
    all_to_all x1, waiting for transfers between devices, per_device(): lax.all_to_all((keep + swapped).reshape(32, 2, 16, WIN), SPREAD, 0, 0)  15.2 us
    pallas_call x1, Pallas kernels, per_device(): modal_call(third_kernel, 4, 4, [MODAL, MODAL, FIELD, FIELD, MODAL, FIELD,...  12.5 us
    all_to_all x1, starting transfers between devices, per_device(): lax.all_to_all((keep + swapped).reshape(32, 2, 16, WIN), SPREAD, 0, 0)  8.65 us
    ppermute x7, waiting for transfers between devices, per_device(): parts.append(lax.ppermute(total, MODE, ring_route(8, k)))  8.33 us
    pallas_call x1, Pallas kernels, per_device(): modal_call(second_kernel, 3, 4, [layer_of(1), STRIP, MODAL] + TABLES, [MO...  7.37 us
    all_to_all x1, starting transfers between devices, per_device(): arrived = lax.all_to_all(pieces, MODE, 0, 0)  7.19 us
  transfers between devices with their start and end apart: 20, of which 8 were waited for; matrix products, arithmetic and copies ran while one was open for 5% of the time, Pallas kernels for 10%

commit v1 on v0

--- a/solution.py
+++ b/solution.py
@@ -20,6 +20,7 @@
 MODE = ("y", "zh")
 SPREAD = ("zl", "x", "y")
 VMEM = pl.BlockSpec(memory_space=pltpu.VMEM)
+HBM = pl.BlockSpec(memory_space=pltpu.HBM)
 SMEM = pl.BlockSpec(memory_space=pltpu.SMEM)
 PARAMS = pltpu.CompilerParams(vmem_limit_bytes=24 * 1024 * 1024)
 
@@ -146,20 +147,38 @@
         out[part] = pltpu.roll(ring, lax.rem(WIN - col, WIN), 1)
 
 
-def prepare_kernel(place, measured, wave, picks, kernel_out, measured_out):
-    def reorder(value):
-        for side in range(2):
-            high, _ = split(value)
-            middle, low = split(value - high.astype(F32))
-            if side == 0:
-                value = mm(picks[0], high) + mm(picks[0], middle) + mm(picks[0], low)
-            else:
-                value = mm(high, picks[1]) + mm(middle, picks[1]) + mm(low, picks[1])
-        return value
-
-    kernel_out[0] = reorder(wave[0])
-    kernel_out[1] = reorder(wave[1])
-    measured_out[...] = reorder(measured[0])
+def reorder(value, picks):
+    for side in range(2):
+        high, _ = split(value)
+        middle, low = split(value - high.astype(F32))
+        if side == 0:
+            value = mm(picks[0], high) + mm(picks[0], middle) + mm(picks[0], low)
+        else:
+            value = mm(high, picks[1]) + mm(middle, picks[1]) + mm(low, picks[1])
+    return value
+
+
+def prepare_kernel(phase, picks, out):
+    angle = reorder(phase[...], picks)
+    out[0] = jnp.cos(angle)
+    out[1] = jnp.sin(angle)
+
+
+def target_kernel(place, measured, picks, out):
+    out[...] = reorder(measured[0], picks)
+
+
+def cut_kernel(place, field, probe, layer0, layer1, half, sem):
+    start = pl.multiple_of(place[2] * HALF, HALF)
+    copies = (
+        pltpu.make_async_copy(field.at[0], layer0, sem.at[0]),
+        pltpu.make_async_copy(probe.at[0, :, pl.ds(start, HALF), :], half, sem.at[1]),
+        pltpu.make_async_copy(field.at[1], layer1, sem.at[2]),
+    )
+    for copy in copies:
+        copy.start()
+    for copy in copies:
+        copy.wait()
 
 
 def spread_mode(pair, window, prop, tables, lane, row_table, mid, out):
@@ -180,21 +199,25 @@
 def start_kernel(place, row_off, col_off, own, halo, probe, prop, tables, lane, row_table,
                  moved, probes, window, mid):
     slot = place[0]
-    cut_window(own.at[0], halo, row_off[slot], col_off[slot], window)
+    cut_window(own, halo, row_off[slot], col_off[slot], window)
     probes[0] = probe[0]
     spread_mode(lambda rows: (probe[0, 0, rows, :], probe[0, 1, rows, :]), window, prop, tables,
                 lane, row_table, mid, moved.at[0])
 
 
-def first_kernel(place, window, mine, other, prop, tables, lane, row_table, moved_in, probes_in,
-                 moved, probes, mid):
-    core = place[2]
+def first_kernel(count, place, window, *refs):
+    mine, other = refs[:count], refs[count : 2 * count]
+    prop, tables, lane, row_table, _, _, moved, probes, mid = refs[2 * count :]
+    core, step = place[2], pl.program_id(0)
 
     def pair(rows):
         index = BLOCKS.index(rows)
         values = []
         for part in range(2):
-            value = jnp.where(core == index, mine[0, part], other[0, part])
+            value = jnp.where(core == index, mine[0][part], other[0][part])
+            if count == 2:
+                later = jnp.where(core == index, mine[1][part], other[1][part])
+                value = jnp.where(step == 0, value, later)
             probes[0, part, rows, :] = value
             values.append(value)
         return values
@@ -208,7 +231,7 @@
 
     @pl.when(pl.program_id(0) == 0)
     def _():
-        cut_window(own.at[0], halo, row_off[slot], col_off[slot], window)
+        cut_window(own, halo, row_off[slot], col_off[slot], window)
         power[...] = jnp.zeros(power.shape, F32)
 
     for rows in BLOCKS:
@@ -228,7 +251,8 @@
 
 def third_kernel(place, row_off, col_off, counts, far, before, window0, window1, probes, prop,
                  power, power_other, measured, tables, lane, row_table,
-                 pieces, keep, send, weight, mid, late, terms):
+                 *rest):
+    pieces, (keep, send, weight, mid, late, terms) = rest[:8], rest[8:]
     slot, core = place[0], place[2]
 
     @pl.when(pl.program_id(0) == 0)
@@ -277,31 +301,34 @@
         for layer in range(2):
             for part in range(2):
                 ring = pltpu.roll(terms[layer, part], row_off[slot], 0)
-                ring = pltpu.roll(ring, col_off[slot], 1)
-                for shard in range(8):
-                    pieces[shard, layer, part] = ring[shard * 32 : shard * 32 + 32]
-
-
-def gather_kernel(place, row_off, col_off, arrived, own, halo):
+                terms[layer, part] = pltpu.roll(ring, col_off[slot], 1)
+        shard = place[0] * 2 + place[1]
+        for step in range(8):
+            start = pl.multiple_of(lax.rem(shard + step, 8) * 32, 32)
+            for layer in range(2):
+                for part in range(2):
+                    pieces[step][layer, part] = terms[layer, part, pl.ds(start, 32), :]
+
+
+def gather_kernel(place, row_off, col_off, *refs):
+    arrived, (own, halo) = refs[:8], refs[8:]
     shard = place[0] * 2 + place[1]
-    rows = lax.broadcasted_iota(jnp.int32, (32, WIN), 0) + shard * 32
+    rows = lax.broadcasted_iota(jnp.int32, (32, HALF), 0) + shard * 32
     lanes = lax.broadcasted_iota(jnp.int32, (32, HALF), 1)
     for layer in range(2):
         for part in range(2):
             mine = [jnp.zeros((32, HALF), F32) for _ in range(3)]
             next_one = [jnp.zeros((32, HALF), F32) for _ in range(3)]
-            for slot in range(4):
-                value = arrived[2 * slot, layer, part] + arrived[2 * slot + 1, layer, part]
+            for step in range(8):
+                slot = lax.div(lax.rem(shard - step + 8, 8), 2)
+                value = arrived[step][layer, part]
+                first, second = value[:, :HALF], value[:, HALF:]
                 inside = rows >= row_off[slot]
                 turned = lanes < col_off[slot]
-                for store, kept in (
-                    (mine, jnp.where(inside, value, 0.0)),
-                    (next_one, jnp.where(inside, 0.0, value)),
-                ):
-                    first, second = kept[:, :HALF], kept[:, HALF:]
-                    store[0] = store[0] + jnp.where(turned, 0.0, first)
-                    store[1] = store[1] + second
-                    store[2] = store[2] + jnp.where(turned, first, 0.0)
+                moves = (jnp.where(turned, 0.0, first), second, jnp.where(turned, first, 0.0))
+                for place_in, move in enumerate(moves):
+                    mine[place_in] = mine[place_in] + jnp.where(inside, move, 0.0)
+                    next_one[place_in] = next_one[place_in] + jnp.where(inside, 0.0, move)
             own[layer, part] = jnp.concatenate(mine, axis=1)
             halo[layer, part] = jnp.concatenate(next_one, axis=1)
 
@@ -337,15 +364,11 @@
     )
 
 
-TABLES = [whole(4, WIN, WIN), whole(2, 8, HALF), whole(2, HALF, HALF)]
+TABLES = [VMEM, VMEM, VMEM]
 PLANE = whole(WIN, WIN)
 FIELD = whole(2, WIN, WIN)
 MODAL = by_mode(2, WIN, WIN)
 STRIP = whole(2, WIN, COLS)
-
-
-def layer_of(layer):
-    return pl.BlockSpec((1, 2, WIN, COLS), lambda *_: (layer, 0, 0, 0))
 
 
 ANY = pl.BlockSpec(memory_space=pl.ANY)
@@ -382,69 +405,82 @@
     back = [(i, i - 1) for i in range(1, 16)]
     ahead = [(i, i + 1) for i in range(15)]
 
-    halo0 = lax.ppermute(object_field[0], TILE, back)
-    half = lax.dynamic_slice_in_dim(probe[0], core * HALF, HALF, axis=1)
-    gathered = []
-    for k in (1, 2, 3):
-        gathered.append(lax.ppermute(half, "y", ring_route(4, k)))
-    later, half = lax.optimization_barrier((object_field, half))
-    halo1 = lax.ppermute(later[1], TILE, back)
+    layer0, layer1, half = pl.pallas_call(
+        cut_kernel,
+        out_shape=(shape(2, WIN, COLS), shape(2, WIN, COLS), shape(2, HALF, WIN)),
+        in_specs=[SMEM, HBM, HBM],
+        out_specs=[VMEM] * 3,
+        scratch_shapes=[pltpu.SemaphoreType.DMA((3,))],
+        compiler_params=PARAMS,
+        name="cut",
+    )(place, *(pltpu.with_memory_space_constraint(v, pltpu.HBM) for v in (object_field, probe)))
+    halo0 = lax.ppermute(layer0, TILE, back)
+    halo1 = lax.ppermute(layer1, TILE, back)
     swap = [(0, 1), (1, 0)]
-    mine13 = jnp.stack([gathered[0], gathered[2]])
-    mine2 = gathered[1][None]
-    other13 = lax.ppermute(mine13, "core", swap)
-    other2 = lax.ppermute(mine2, "core", swap)
-
-    wave = jnp.stack([jnp.cos(prop_phase), jnp.sin(prop_phase)])
-    prop, target = pl.pallas_call(
+    mine, other = {}, {}
+    for k in (1, 3, 2):
+        mine[k] = lax.ppermute(half, "y", ring_route(4, k))
+        other[k] = lax.ppermute(mine[k], "core", swap)
+
+    prop = pl.pallas_call(
         prepare_kernel,
-        out_shape=(shape(2, WIN, WIN), shape(WIN, WIN)),
+        out_shape=shape(2, WIN, WIN),
+        in_specs=[VMEM, VMEM],
+        out_specs=VMEM,
+        compiler_params=PARAMS,
+        name="prepare",
+    )(prop_phase, picks)
+    target = pl.pallas_call(
+        target_kernel,
+        out_shape=shape(WIN, WIN),
         grid_spec=pltpu.PrefetchScalarGridSpec(
             num_scalar_prefetch=1,
             grid=(1,),
-            in_specs=[
-                pl.BlockSpec((1, WIN, WIN), lambda i, p: (p[0], 0, 0)), FIELD, FIELD
-            ],
-            out_specs=[FIELD, PLANE],
+            in_specs=[pl.BlockSpec((1, WIN, WIN), lambda i, p: (p[0], 0, 0)), VMEM],
+            out_specs=PLANE,
         ),
         compiler_params=PARAMS,
-        name="prepare",
-    )(place, measured, wave, picks)
+        name="target",
+    )(place, measured, picks)
 
     modes = shape(4, 2, WIN, WIN)
     tables = (matrices, lane_table, row_table)
     work = [pltpu.VMEM((2, WIN, WIN), F32)]
     moved, probes, window0 = modal_call(
         start_kernel, 3, 1,
-        [layer_of(0), STRIP, MODAL, FIELD] + TABLES,
+        [STRIP, STRIP, MODAL, FIELD] + TABLES,
         [MODAL, MODAL, FIELD], (modes, modes, shape(2, WIN, WIN)), work,
-    )(place, row_offset, col_offset, object_field, halo0, probe, prop, *tables)
-    for base, mine, other in ((1, mine13, other13), (2, mine2, other2)):
+    )(place, row_offset, col_offset, layer0, halo0, probe, prop, *tables)
+    for steps in ((1, 3), (2,)):
+        count = len(steps)
         target_block = pl.BlockSpec(
-            (1, 2, WIN, WIN), lambda i, *_, base=base: (base + 2 * i, 0, 0, 0)
+            (1, 2, WIN, WIN), lambda i, *_, base=steps[0]: (base + 2 * i, 0, 0, 0)
         )
         moved, probes = modal_call(
-            first_kernel, 1, mine.shape[0],
-            [FIELD, by_mode(2, HALF, WIN), by_mode(2, HALF, WIN), FIELD] + TABLES + [ANY, ANY],
-            [target_block, target_block], (modes, modes), work, {8: 0, 9: 1},
-        )(place, window0, mine, other, prop, *tables, moved, probes)
+            functools.partial(first_kernel, count), 1, count,
+            [VMEM] * (2 * count + 2) + TABLES + [ANY, ANY],
+            [target_block, target_block], (modes, modes), work,
+            {2 * count + 6: 0, 2 * count + 7: 1},
+        )(place, window0, *[mine[k] for k in steps], *[other[k] for k in steps], prop,
+          *tables, moved, probes)
 
     before, far, power, window1 = modal_call(
         second_kernel, 3, 4,
-        [layer_of(1), STRIP, MODAL] + TABLES,
+        [STRIP, STRIP, MODAL] + TABLES,
         [MODAL, MODAL, PLANE, FIELD],
         (modes, modes, shape(WIN, WIN), shape(2, WIN, WIN)),
         work,
-    )(place, row_offset, col_offset, object_field, halo1, moved, *tables)
+    )(place, row_offset, col_offset, layer1, halo1, moved, *tables)
 
     power_other = lax.ppermute(power, "zh", [(0, 1), (1, 0)])
 
     parts_shape = shape(8, 4, 2, 16, WIN)
-    pieces, keep, send = modal_call(
+    piece = shape(2, 2, 32, WIN)
+    *pieces, keep, send = modal_call(
         third_kernel, 4, 4,
-        [MODAL, MODAL, FIELD, FIELD, MODAL, FIELD, PLANE, PLANE, PLANE] + TABLES,
-        [whole(8, 2, 2, 32, WIN), by_home(), by_home()],
-        (shape(8, 2, 2, 32, WIN), parts_shape, parts_shape),
+        [MODAL, MODAL, VMEM, VMEM, MODAL] + [VMEM] * 4 + TABLES,
+        [whole(2, 2, 32, WIN)] * 8 + [by_home(), by_home()],
+        (piece,) * 8 + (parts_shape, parts_shape),
         [
             pltpu.VMEM((WIN, WIN), F32),
             pltpu.VMEM((2, WIN, WIN), F32),
@@ -455,18 +491,21 @@
       power_other, target, *tables)
 
     swapped = lax.ppermute(send, "core", [(0, 1), (1, 0)])
-    arrived = lax.all_to_all(pieces, MODE, 0, 0)
+    arrived = [pieces[0]]
+    for k in range(1, 8):
+        arrived.append(lax.ppermute(pieces[k], MODE, ring_route(8, k)))
+    kept = keep + swapped
+    spread = lax.all_to_all(kept.reshape(32, 2, 16, WIN), SPREAD, 0, 0)
+    probe_part = jnp.sum(spread, axis=0)
     own, over = pl.pallas_call(
         gather_kernel,
         out_shape=(shape(2, 2, 32, COLS), shape(2, 2, 32, COLS)),
-        in_specs=[SMEM] * 3 + [VMEM],
+        in_specs=[SMEM] * 3 + [VMEM] * 8,
         out_specs=[VMEM] * 2,
         compiler_params=PARAMS,
         name="gather",
-    )(place, row_offset, col_offset, arrived)
+    )(place, row_offset, col_offset, *arrived)
     over_in = lax.ppermute(over, TILE, ahead)
-    spread = lax.all_to_all((keep + swapped).reshape(32, 2, 16, WIN), SPREAD, 0, 0)
-    probe_part = jnp.sum(spread, axis=0)
 
     total = own + over_in
     parts = []

time: 159 us -> 149 us (0.937); the launches traced: 156 us -> 148 us
  starting transfers between devices: 52.6 us -> 63.7 us
  local copies, waits for them, and re-layouts: 11.3 us -> 1.74 us
  waiting for transfers between devices: 52.6 us -> 45.3 us
    all_to_all x2 -> x1, waiting for transfers between devices: 31.3 us -> 0.01 us  [per_device(): spread = lax.all_to_all(kept.reshape(32, 2, 16, WIN), SPREAD, 0, 0)]
    ppermute x7 -> x15, waiting for transfers between devices: 7.13 us -> 27.3 us  [the longest x7 18 us: per_device(): arrived.append(lax.ppermute(pieces[k], MODE, ring_route(8, k)))]
    ppermute x7 -> x15, starting transfers between devices: 9.12 us -> 26.5 us  [the longest x7 16 us: per_device(): arrived.append(lax.ppermute(pieces[k], MODE, ring_route(8, k)))]
    all_to_all x2 -> x1, starting transfers between devices: 15.8 us -> 8.22 us  [per_device(): spread = lax.all_to_all(kept.reshape(32, 2, 16, WIN), SPREAD, 0, 0)]
    unnamed x26 -> x18, local copies, waits for them, and re-layouts: 3.87 us -> 0.05 us
    squeeze x2 -> x0, local copies, waits for them, and re-layouts: 3.01 us -> none  [the longest x1 2.08 us: per_device(): halo0 = lax.ppermute(object_field[0], TILE, back)]
    ppermute x1, waiting for transfers between devices: 0.01 us -> 2.65 us  [per_device(): swapped = lax.ppermute(send, 'core', [(0, 1), (1, 0)])]
    all_to_all x1, starting transfers between devices: 3.57 us -> 6.05 us  [per_device(): lax.all_to_all(jnp.broadcast_to(probe_part, (16, 2, 16, WIN)), TILE, 0, 0)]
  transfers between devices with their start and end apart: 20 -> 27, of which waited for: 8 -> 13; matrix products, arithmetic and copies ran while one was open for 5% -> 1% of each run, Pallas kernels for 10% -> 9%
where the time goes in v1:
time: 149 us; the launch traced here: 148 us
  starting transfers between devices  63.7 us (43%)
  waiting for transfers between devices  45.3 us (30%)
  Pallas kernels  34.2 us (23%)
  local copies, waits for them, and re-layouts  1.74 us (1%)
  between operations  1.65 us (1%)
    ppermute x7, waiting for transfers between devices, per_device(): arrived.append(lax.ppermute(pieces[k], MODE, ring_route(8, k)))  18 us
    ppermute x7, starting transfers between devices, per_device(): parts.append(lax.ppermute(total, MODE, ring_route(8, k)))  17.4 us
    ppermute x7, starting transfers between devices, per_device(): arrived.append(lax.ppermute(pieces[k], MODE, ring_route(8, k)))  16 us
    pallas_call x1, Pallas kernels, per_device(): modal_call(third_kernel, 4, 4, [MODAL, MODAL, VMEM, VMEM, MODAL] + [VMEM]...  12.1 us
    ppermute x7, waiting for transfers between devices, per_device(): parts.append(lax.ppermute(total, MODE, ring_route(8, k)))  10.7 us
    ppermute x3, waiting for transfers between devices, per_device(): mine[k] = lax.ppermute(half, 'y', ring_route(4, k))  9.33 us
    all_to_all x1, starting transfers between devices, per_device(): spread = lax.all_to_all(kept.reshape(32, 2, 16, WIN), SPREAD, 0, 0)  8.22 us
    pallas_call x1, Pallas kernels, per_device(): modal_call(second_kernel, 3, 4, [STRIP, STRIP, MODAL] + TABLES, [MODAL, M...  6.19 us
  transfers between devices with their start and end apart: 27, of which 13 were waited for; matrix products, arithmetic and copies ran while one was open for 1% of the time, Pallas kernels for 9%

profile of v1, /device:TPU:0, one launch (start us, length us, event | category | flops | bytes accessed | tf_op | source)
XLA Modules:
  0.0 148.0 jit_solution(10613157431672278268)
XLA Ops:
  0.6 0.0 copy-start.4
  0.6 0.0 copy-start
  0.7 0.0 copy-start.6
  0.7 0.0 copy-start.1
  0.7 0.0 copy-start.2
  0.7 0.1 pad_add_fusion.place
  0.8 2.0 %cut.1 = (f32[2,256,384]{2,1,0:T(8,128)S(1)}, f32[2,256,384]{2,1,0:T(8,128)S(1)}, f32[2,128,256]{2,1,0:T(8,128)S(1)}) custom-call(s32[3]{0:T(128)S(1)} %pad_add_fusion.place, f32[2,2,256,384]{3,2,1,0:T(8,128)} %field.1, f32[1,2,256,256]{3,2,1,0:T(8,128)} %probe.3), custom_call_target="tpu_custom_call" | custom-call | tf_op jit(solution)/shard_map/cut/pallas_call | solution.py:408
  2.8 1.3 collective-permute-start.1
  4.1 1.3 collective-permute-start
  5.4 1.8 %collective-permute-start.4 = (f32[2,128,256]{2,1,0:T(8,128)S(1)}, f32[2,128,256]{2,1,0:T(8,128)S(1)}, u32[]{:S(2)}, u32[]{:S(2)}) collective-permute-start(f32[2,128,256]{2,1,0:T(8,128)S(1)} %get-tuple-element.31), channel_id=1, source_target_pairs={{0,2},{2,4},{4,6},{6,0},{1,3},{3,5},{5,7},{7,1},{8,10},{10,12},{12... | collective-permute-start | bytes 786440 | tf_op jit(solution)/shard_map/ppermute | solution.py:422
  7.2 1.5 %collective-permute-start.5 = (f32[2,128,256]{2,1,0:T(8,128)S(1)}, f32[2,128,256]{2,1,0:T(8,128)S(1)}, u32[]{:S(2)}, u32[]{:S(2)}) collective-permute-start(f32[2,128,256]{2,1,0:T(8,128)S(1)} %get-tuple-element.31), channel_id=1, source_target_pairs={{0,6},{2,0},{4,2},{6,4},{1,7},{3,1},{5,3},{7,5},{8,14},{10,8},{12,... | collective-permute-start | bytes 786440 | tf_op jit(solution)/shard_map/ppermute | solution.py:422
  8.7 2.1 %collective-permute-start.2 = (f32[2,128,256]{2,1,0:T(8,128)S(1)}, f32[2,128,256]{2,1,0:T(8,128)S(1)}, u32[]{:S(2)}, u32[]{:S(2)}) collective-permute-start(f32[2,128,256]{2,1,0:T(8,128)S(1)} %get-tuple-element.31), channel_id=1, source_target_pairs={{0,4},{2,6},{4,0},{6,2},{1,5},{3,7},{5,1},{7,3},{8,12},{10,14},{12... | collective-permute-start | bytes 786440 | tf_op jit(solution)/shard_map/ppermute | solution.py:422
  10.8 4.1 %collective-permute-done.4.refs_0_ = f32[2,128,256]{2,1,0:T(8,128)S(1)} collective-permute-done((f32[2,128,256]{2,1,0:T(8,128)S(1)}, f32[2,128,256]{2,1,0:T(8,128)S(1)}, u32[]{:S(2)}, u32[]{:S(2)}) %collective-permute-start.4) | collective-permute-done | bytes 262176 | tf_op jit(solution)/shard_map/ppermute | solution.py:422
  14.9 0.8 collective-permute-start.6
  15.7 0.1 collective-permute-done.5.refs_1_
  15.9 1.1 collective-permute-start.7
  17.0 5.1 %collective-permute-done.2.refs_0_ = f32[2,128,256]{2,1,0:T(8,128)S(1)} collective-permute-done((f32[2,128,256]{2,1,0:T(8,128)S(1)}, f32[2,128,256]{2,1,0:T(8,128)S(1)}, u32[]{:S(2)}, u32[]{:S(2)}) %collective-permute-start.2) | collective-permute-done | bytes 262176 | tf_op jit(solution)/shard_map/ppermute | solution.py:422
  22.1 0.6 collective-permute-start.3
  22.7 1.5 prepare.1.prop.refs_4_.refs_2_
  24.1 0.0 collective-permute-done.1.halo
  24.2 2.3 %shard_map.122 = (f32[4,2,256,256]{3,2,1,0:T(8,128)S(1)}, f32[4,2,256,256]{3,2,1,0:T(8,128)S(1)}, f32[2,256,256]{2,1,0:T(8,128)S(1)}) custom-call(s32[3]{0:T(128)S(1)} %pad_add_fusion.place, s32[4]{0:T(128)S(1)} %copy-done.7, s32[4]{0:T(128)S(1)} %copy-done.8, f32[2,256,384]{2,1,0:T(8,128)S(1)} %get-tuple-element.29.own, ...), custom_call_target="tpu_custom_call" | custom-call | tf_op jit(solution)/shard_map/pallas_call | solution.py:449
  26.6 0.0 collective-permute-done.7.refs_3_
  26.6 3.3 %shard_map.123 = (f32[4,2,256,256]{3,2,1,0:T(8,128)S(1)}, f32[4,2,256,256]{3,2,1,0:T(8,128)S(1)}) custom-call(s32[3]{0:T(128)S(1)} %pad_add_fusion.place, f32[2,256,256]{2,1,0:T(8,128)S(1)} %get-tuple-element.30.window.window0, f32[2,128,256]{2,1,0:T(8,128)S(1)} %collective-permute-done.4.refs_0_, ...), custom_call_target="tpu_custom_call", output_to_operand_aliasing={{0}: (10, {}), {1}: (11, {})} | custom-call | tf_op jit(solution)/shard_map/pallas_call | solution.py:459
  29.9 1.9 %shard_map.124 = (f32[4,2,256,256]{3,2,1,0:T(8,128)S(1)}, f32[4,2,256,256]{3,2,1,0:T(8,128)S(1)}) custom-call(s32[3]{0:T(128)S(1)} %pad_add_fusion.place, f32[2,256,256]{2,1,0:T(8,128)S(1)} %get-tuple-element.30.window.window0, f32[2,128,256]{2,1,0:T(8,128)S(1)} %collective-permute-done.2.refs_0_, ...), custom_call_target="tpu_custom_call", output_to_operand_aliasing={{0}: (8, {}), {1}: (9, {})} | custom-call | tf_op jit(solution)/shard_map/pallas_call | solution.py:459
  31.7 0.0 copy-start.3
  31.7 6.2 %shard_map.125 = (f32[4,2,256,256]{3,2,1,0:T(8,128)S(1)}, f32[4,2,256,256]{3,2,1,0:T(8,128)S(1)}, f32[256,256]{1,0:T(8,128)S(1)}, f32[2,256,256]{2,1,0:T(8,128)S(1)}) custom-call(s32[3]{0:T(128)S(1)} %pad_add_fusion.place, s32[4]{0:T(128)S(1)} %copy-done.7, s32[4]{0:T(128)S(1)} %copy-done.8, f32[2,256,384]{2,1,0:T(8,128)S(1)} %get-tuple-element.28.own, ...), custom_call_target="tpu_custom_call" | custom-call | tf_op jit(solution)/shard_map/pallas_call | solution.py:467
  37.9 4.0 %collective-permute-start.8 = (f32[256,256]{1,0:T(8,128)S(1)}, f32[256,256]{1,0:T(8,128)S(1)}, u32[]{:S(2)}, u32[]{:S(2)}) collective-permute-start(f32[256,256]{1,0:T(8,128)S(1)} %get-tuple-element.41.power), channel_id=1, source_target_pairs={{0,1},{1,0},{2,3},{3,2},{4,5},{5,4},{6,7},{7,6},{8,9},{9,8},{10,11... | collective-permute-start | bytes 786440 | tf_op jit(solution)/shard_map/ppermute | solution.py:475
  41.9 1.2 target.1.measured
  43.7 4.7 %collective-permute-done.8.power_other = f32[256,256]{1,0:T(8,128)S(1)} collective-permute-done((f32[256,256]{1,0:T(8,128)S(1)}, f32[256,256]{1,0:T(8,128)S(1)}, u32[]{:S(2)}, u32[]{:S(2)}) %collective-permute-start.8) | collective-permute-done | bytes 262176 | tf_op jit(solution)/shard_map/ppermute | solution.py:475
  48.4 12.1 %shard_map.126 = (f32[2,2,32,256]{3,2,1,0:T(8,128)S(1)}, f32[2,2,32,256]{3,2,1,0:T(8,128)S(1)}, f32[2,2,32,256]{3,2,1,0:T(8,128)S(1)}, f32[2,2,32,256]{3,2,1,0:T...) custom-call(s32[3]{0:T(128)S(1)} %pad_add_fusion.place, ...), custom_call_target="tpu_custom_call" | custom-call | tf_op jit(solution)/shard_map/pallas_call | solution.py:479
  60.5 0.3 collective-permute-start.24
  60.7 2.6 %collective-permute-done.24 = f32[8,4,2,16,256]{4,3,2,1,0:T(8,128)S(1)} collective-permute-done((f32[8,4,2,16,256]{4,3,2,1,0:T(8,128)S(1)}, f32[8,4,2,16,256]{4,3,2,1,0:T(8,128)S(1)}, u32[]{:S(2)}, u32[]{:S(2)}) %collective-permute-start.24) | collective-permute-done | bytes 1048608 | tf_op jit(solution)/shard_map/ppermute | solution.py:493
  63.4 1.2 add.7
  64.6 8.2 %all-to-all-start = ((f32[32,2,16,256]{3,2,1,0:T(8,128)}), f32[32,2,16,256]{3,2,1,0:T(8,128)S(1)}, u32[]{:S(2)}, u32[]{:S(2)}) async-start(f32[32,2,16,256]{3,2,1,0:T(8,128)} %bitcast.3), calls=%async_computation | async-start | bytes 2097152 | tf_op jit(solution)/shard_map/all_to_all | solution.py:498
  72.8 1.9 %collective-permute-start.10 = (f32[2,2,32,256]{3,2,1,0:T(8,128)S(1)}, f32[2,2,32,256]{3,2,1,0:T(8,128)S(1)}, u32[]{:S(2)}, u32[]{:S(2)}) collective-permute-start(f32[2,2,32,256]{3,2,1,0:T(8,128)S(1)} %get-tuple-element.44), channel_id=1, source_target_pairs={{0,2},{1,3},{2,4},{3,5},{4,6},{5,7},{6,0},{7,1},{8,10},{9,11},{10,... | collective-permute-start | bytes 393224 | tf_op jit(solution)/shard_map/ppermute | solution.py:496
  74.7 4.5 %collective-permute-start.11 = (f32[2,2,32,256]{3,2,1,0:T(8,128)S(1)}, f32[2,2,32,256]{3,2,1,0:T(8,128)S(1)}, u32[]{:S(2)}, u32[]{:S(2)}) collective-permute-start(f32[2,2,32,256]{3,2,1,0:T(8,128)S(1)} %get-tuple-element.45), channel_id=1, source_target_pairs={{0,3},{1,4},{2,5},{3,6},{4,7},{5,0},{6,1},{7,2},{8,11},{9,12},{10,... | collective-permute-start | bytes 393224 | tf_op jit(solution)/shard_map/ppermute | solution.py:496
  79.1 1.4 collective-permute-start.12
  80.6 2.7 %collective-permute-start.13 = (f32[2,2,32,256]{3,2,1,0:T(8,128)S(1)}, f32[2,2,32,256]{3,2,1,0:T(8,128)S(1)}, u32[]{:S(2)}, u32[]{:S(2)}) collective-permute-start(f32[2,2,32,256]{3,2,1,0:T(8,128)S(1)} %get-tuple-element.47), channel_id=1, source_target_pairs={{0,5},{1,6},{2,7},{3,0},{4,1},{5,2},{6,3},{7,4},{8,13},{9,14},{10,... | collective-permute-start | bytes 393224 | tf_op jit(solution)/shard_map/ppermute | solution.py:496
  83.3 1.5 collective-permute-start.14
  84.7 6.4 %collective-permute-done.10.refs_2_ = f32[2,2,32,256]{3,2,1,0:T(8,128)S(1)} collective-permute-done((f32[2,2,32,256]{3,2,1,0:T(8,128)S(1)}, f32[2,2,32,256]{3,2,1,0:T(8,128)S(1)}, u32[]{:S(2)}, u32[]{:S(2)}) %collective-permute-start.10) | collective-permute-done | bytes 131104 | tf_op jit(solution)/shard_map/ppermute | solution.py:496
  91.1 4.1 %collective-permute-start.15 = (f32[2,2,32,256]{3,2,1,0:T(8,128)S(1)}, f32[2,2,32,256]{3,2,1,0:T(8,128)S(1)}, u32[]{:S(2)}, u32[]{:S(2)}) collective-permute-start(f32[2,2,32,256]{3,2,1,0:T(8,128)S(1)} %get-tuple-element.49), channel_id=1, source_target_pairs={{0,7},{1,0},{2,1},{3,2},{4,3},{5,4},{6,5},{7,6},{8,15},{9,8},{10,9... | collective-permute-start | bytes 393224 | tf_op jit(solution)/shard_map/ppermute | solution.py:496
  95.2 3.0 %collective-permute-done.11.refs_3_ = f32[2,2,32,256]{3,2,1,0:T(8,128)S(1)} collective-permute-done((f32[2,2,32,256]{3,2,1,0:T(8,128)S(1)}, f32[2,2,32,256]{3,2,1,0:T(8,128)S(1)}, u32[]{:S(2)}, u32[]{:S(2)}) %collective-permute-start.11) | collective-permute-done | bytes 131104 | tf_op jit(solution)/shard_map/ppermute | solution.py:496
  98.2 0.0 collective-permute-start.9
  98.3 0.0 collective-permute-done.12.refs_4_
  98.3 1.1 collective-permute-done.13.refs_5_
  99.3 2.2 %collective-permute-done.15.refs_7_ = f32[2,2,32,256]{3,2,1,0:T(8,128)S(1)} collective-permute-done((f32[2,2,32,256]{3,2,1,0:T(8,128)S(1)}, f32[2,2,32,256]{3,2,1,0:T(8,128)S(1)}, u32[]{:S(2)}, u32[]{:S(2)}) %collective-permute-start.15) | collective-permute-done | bytes 131104 | tf_op jit(solution)/shard_map/ppermute | solution.py:496
  101.5 5.3 %collective-permute-done.9.refs_1_ = f32[2,2,32,256]{3,2,1,0:T(8,128)S(1)} collective-permute-done((f32[2,2,32,256]{3,2,1,0:T(8,128)S(1)}, f32[2,2,32,256]{3,2,1,0:T(8,128)S(1)}, u32[]{:S(2)}, u32[]{:S(2)}) %collective-permute-start.9) | collective-permute-done | bytes 131104 | tf_op jit(solution)/shard_map/ppermute | solution.py:496
  106.8 0.9 gather.1
  107.7 1.3 collective-permute-start.16
  109.0 0.1 reduce_sum.9
  109.1 0.9 broadcast_in_dim.3
  109.9 6.1 %all-to-all-start.1 = ((f32[16,2,16,256]{3,2,1,0:T(8,128)}), f32[16,2,16,256]{3,2,1,0:T(8,128)S(1)}, u32[]{:S(2)}, u32[]{:S(2)}) async-start(f32[16,2,16,256]{3,2,1,0:T(8,128)} %broadcast_in_dim.3), calls=%async_computation.1 | async-start | bytes 1048576 | tf_op jit(solution)/shard_map/all_to_all | solution.py:514
  116.1 0.8 collective-permute-start.17
  116.9 3.8 %collective-permute-start.19 = (f32[2,2,32,384]{3,2,1,0:T(8,128)S(1)}, f32[2,2,32,384]{3,2,1,0:T(8,128)S(1)}, u32[]{:S(2)}, u32[]{:S(2)}) collective-permute-start(f32[2,2,32,384]{3,2,1,0:T(8,128)S(1)} %add.6.refs_0_), channel_id=1, source_target_pairs={{0,3},{1,4},{2,5},{3,6},{4,7},{5,0},{6,1},{7,2},{8,11},{9,12},{10,... | collective-permute-start | bytes 589832 | tf_op jit(solution)/shard_map/ppermute | solution.py:513
  120.7 2.5 %collective-permute-start.20 = (f32[2,2,32,384]{3,2,1,0:T(8,128)S(1)}, f32[2,2,32,384]{3,2,1,0:T(8,128)S(1)}, u32[]{:S(2)}, u32[]{:S(2)}) collective-permute-start(f32[2,2,32,384]{3,2,1,0:T(8,128)S(1)} %add.6.refs_0_), channel_id=1, source_target_pairs={{0,4},{1,5},{2,6},{3,7},{4,0},{5,1},{6,2},{7,3},{8,12},{9,13},{10,... | collective-permute-start | bytes 589832 | tf_op jit(solution)/shard_map/ppermute | solution.py:513
  123.2 1.8 %collective-permute-start.21 = (f32[2,2,32,384]{3,2,1,0:T(8,128)S(1)}, f32[2,2,32,384]{3,2,1,0:T(8,128)S(1)}, u32[]{:S(2)}, u32[]{:S(2)}) collective-permute-start(f32[2,2,32,384]{3,2,1,0:T(8,128)S(1)} %add.6.refs_0_), channel_id=1, source_target_pairs={{0,5},{1,6},{2,7},{3,0},{4,1},{5,2},{6,3},{7,4},{8,13},{9,14},{10,... | collective-permute-start | bytes 589832 | tf_op jit(solution)/shard_map/ppermute | solution.py:513
  125.0 6.0 %collective-permute-done.17.refs_0_ = f32[2,2,32,384]{3,2,1,0:T(8,128)S(1)} collective-permute-done((f32[2,2,32,384]{3,2,1,0:T(8,128)S(1)}, f32[2,2,32,384]{3,2,1,0:T(8,128)S(1)}, u32[]{:S(2)}, u32[]{:S(2)}) %collective-permute-start.17) | collective-permute-done | bytes 196640 | tf_op jit(solution)/shard_map/ppermute | solution.py:513
  131.1 5.0 %collective-permute-start.22 = (f32[2,2,32,384]{3,2,1,0:T(8,128)S(1)}, f32[2,2,32,384]{3,2,1,0:T(8,128)S(1)}, u32[]{:S(2)}, u32[]{:S(2)}) collective-permute-start(f32[2,2,32,384]{3,2,1,0:T(8,128)S(1)} %add.6.refs_0_), channel_id=1, source_target_pairs={{0,6},{1,7},{2,0},{3,1},{4,2},{5,3},{6,4},{7,5},{8,14},{9,15},{10,... | collective-permute-start | bytes 589832 | tf_op jit(solution)/shard_map/ppermute | solution.py:513
  136.0 3.4 %collective-permute-start.23 = (f32[2,2,32,384]{3,2,1,0:T(8,128)S(1)}, f32[2,2,32,384]{3,2,1,0:T(8,128)S(1)}, u32[]{:S(2)}, u32[]{:S(2)}) collective-permute-start(f32[2,2,32,384]{3,2,1,0:T(8,128)S(1)} %add.6.refs_0_), channel_id=1, source_target_pairs={{0,7},{1,0},{2,1},{3,2},{4,3},{5,4},{6,5},{7,6},{8,15},{9,8},{10,9... | collective-permute-start | bytes 589832 | tf_op jit(solution)/shard_map/ppermute | solution.py:513
  139.5 1.3 joina.1.refs_7_
  140.8 0.5 collective-permute-done.21.refs_4_
  141.3 4.1 %collective-permute-done.23.refs_6_ = f32[2,2,32,384]{3,2,1,0:T(8,128)S(1)} collective-permute-done((f32[2,2,32,384]{3,2,1,0:T(8,128)S(1)}, f32[2,2,32,384]{3,2,1,0:T(8,128)S(1)}, u32[]{:S(2)}, u32[]{:S(2)}) %collective-permute-start.23) | collective-permute-done | bytes 196640 | tf_op jit(solution)/shard_map/ppermute | solution.py:513
  145.4 1.7 %joinb.1 = f32[2,2,256,384]{3,2,1,0:T(8,128)} custom-call(s32[3]{0:T(128)S(1)} %pad_add_fusion.place, f32[2,2,32,384]{3,2,1,0:T(8,128)S(1)} %collective-permute-done.17.refs_0_, f32[2,2,32,384]{3,2,1,0:T(8,128)S(1)} %collective-permute-done.18.refs_1_, f32[2,2,32,384]{3,2,1,0:T(8,128)S(1)} %collective-permute-done.19.refs_2_, ...), custom_call_target="tpu_custom_call", output_to_operand_aliasing={{}: (8, {})} | custom-call | tf_op jit(solution)/shard_map/joinb/pallas_call | solution.py:524
  147.1 0.8 copy.18
  (25 shorter events, 0.1 us)
Async XLA Ops:
  0.6 22.1 %copy-start.4 = (bf16[2,256,256]{2,1,0:T(8,128)(2,1)S(1)}, bf16[2,256,256]{2,1,0:T(8,128)(2,1)}, u32[]{:S(2)}) copy-start(bf16[2,256,256]{2,1,0:T(8,128)(2,1)} %constant.24.clone.picks) | copy-start | bytes 786436
  0.6 23.5 %copy-start = (bf16[4,256,256]{2,1,0:T(8,128)(2,1)S(1)}, bf16[4,256,256]{2,1,0:T(8,128)(2,1)}, u32[]{:S(2)}) copy-start(bf16[4,256,256]{2,1,0:T(8,128)(2,1)} %constant.21.clone.tables.refs_5_.refs_3_) | copy-start | bytes 1572868
  0.7 23.5 %copy-start.6 = (f32[2,8,128]{2,1,0:T(8,128)S(1)}, f32[2,8,128]{2,1,0:T(8,128)}, u32[]{:S(2)}) copy-start(f32[2,8,128]{2,1,0:T(8,128)} %constant.22.clone.lane.refs_6_.refs_4_) | copy-start | bytes 24580
  0.7 23.5 %copy-start.1 = (f32[2,128,128]{2,1,0:T(8,128)S(1)}, f32[2,128,128]{2,1,0:T(8,128)}, u32[]{:S(2)}) copy-start(f32[2,128,128]{2,1,0:T(8,128)} %constant.23.clone.row_table.refs_7_.refs_5_) | copy-start | bytes 393220
  0.7 23.5 %copy-start.2 = (f32[1,2,256,256]{3,2,1,0:T(8,128)S(1)}, f32[1,2,256,256]{3,2,1,0:T(8,128)}, u32[]{:S(2)}) copy-start(f32[1,2,256,256]{3,2,1,0:T(8,128)} %probe.3) | copy-start | bytes 1572868
  0.7 22.0 %copy-start.5 = (f32[256,256]{1,0:T(8,128)S(1)}, f32[256,256]{1,0:T(8,128)}, u32[]{:S(2)}) copy-start(f32[256,256]{1,0:T(8,128)} %phase.1) | copy-start | bytes 786436
  0.7 23.5 %copy-start.7 = (s32[4]{0:T(128)S(1)}, s32[4]{0:T(128)}, u32[]{:S(2)}) copy-start(s32[4]{0:T(128)} %row_off.7) | copy-start | bytes 52
  0.7 23.5 %copy-start.8 = (s32[4]{0:T(128)S(1)}, s32[4]{0:T(128)}, u32[]{:S(2)}) copy-start(s32[4]{0:T(128)} %col_off.7) | copy-start | bytes 52
  2.8 21.3 %collective-permute-start.1 = (f32[2,256,384]{2,1,0:T(8,128)S(1)}, f32[2,256,384]{2,1,0:T(8,128)S(1)}, u32[]{:S(2)}, u32[]{:S(2)}) collective-permute-start(f32[2,256,384]{2,1,0:T(8,128)S(1)} %get-tuple-element.29.own), channel_id=1, source_target_pairs={{8,0},{16,8},{24,16},{32,24},{40,32},{48,40},{56,48},{64,56},{72,6... | collective-permute-start | bytes 2359304 | tf_op jit(solution)/shard_map/ppermute | solution.py:417
  4.1 27.6 %collective-permute-start = (f32[2,256,384]{2,1,0:T(8,128)S(1)}, f32[2,256,384]{2,1,0:T(8,128)S(1)}, u32[]{:S(2)}, u32[]{:S(2)}) collective-permute-start(f32[2,256,384]{2,1,0:T(8,128)S(1)} %get-tuple-element.28.own), channel_id=1, source_target_pairs={{8,0},{16,8},{24,16},{32,24},{40,32},{48,40},{56,48},{64,56},{72,6... | collective-permute-start | bytes 2359304 | tf_op jit(solution)/shard_map/ppermute | solution.py:418
  5.4 9.5 %collective-permute-start.4 = (f32[2,128,256]{2,1,0:T(8,128)S(1)}, f32[2,128,256]{2,1,0:T(8,128)S(1)}, u32[]{:S(2)}, u32[]{:S(2)}) collective-permute-start(f32[2,128,256]{2,1,0:T(8,128)S(1)} %get-tuple-element.31), channel_id=1, source_target_pairs={{0,2},{2,4},{4,6},{6,0},{1,3},{3,5},{5,7},{7,1},{8,10},{10,12},{12... | collective-permute-start | bytes 786440 | tf_op jit(solution)/shard_map/ppermute | solution.py:422
  7.2 8.7 %collective-permute-start.5 = (f32[2,128,256]{2,1,0:T(8,128)S(1)}, f32[2,128,256]{2,1,0:T(8,128)S(1)}, u32[]{:S(2)}, u32[]{:S(2)}) collective-permute-start(f32[2,128,256]{2,1,0:T(8,128)S(1)} %get-tuple-element.31), channel_id=1, source_target_pairs={{0,6},{2,0},{4,2},{6,4},{1,7},{3,1},{5,3},{7,5},{8,14},{10,8},{12,... | collective-permute-start | bytes 786440 | tf_op jit(solution)/shard_map/ppermute | solution.py:422
  8.7 13.3 %collective-permute-start.2 = (f32[2,128,256]{2,1,0:T(8,128)S(1)}, f32[2,128,256]{2,1,0:T(8,128)S(1)}, u32[]{:S(2)}, u32[]{:S(2)}) collective-permute-start(f32[2,128,256]{2,1,0:T(8,128)S(1)} %get-tuple-element.31), channel_id=1, source_target_pairs={{0,4},{2,6},{4,0},{6,2},{1,5},{3,7},{5,1},{7,3},{8,12},{10,14},{12... | collective-permute-start | bytes 786440 | tf_op jit(solution)/shard_map/ppermute | solution.py:422
  14.9 11.6 %collective-permute-start.6 = (f32[2,128,256]{2,1,0:T(8,128)S(1)}, f32[2,128,256]{2,1,0:T(8,128)S(1)}, u32[]{:S(2)}, u32[]{:S(2)}) collective-permute-start(f32[2,128,256]{2,1,0:T(8,128)S(1)} %collective-permute-done.4.refs_0_), channel_id=1, source_target_pairs={{0,8},{8,0},{1,9},{9,1},{2,10},{10,2},{3,11},{11,3},{4,12},{12,4},... | collective-permute-start | bytes 786440 | tf_op jit(solution)/shard_map/ppermute | solution.py:423
  15.9 10.7 %collective-permute-start.7 = (f32[2,128,256]{2,1,0:T(8,128)S(1)}, f32[2,128,256]{2,1,0:T(8,128)S(1)}, u32[]{:S(2)}, u32[]{:S(2)}) collective-permute-start(f32[2,128,256]{2,1,0:T(8,128)S(1)} %collective-permute-done.5.refs_1_), channel_id=1, source_target_pairs={{0,8},{8,0},{1,9},{9,1},{2,10},{10,2},{3,11},{11,3},{4,12},{12,4},... | collective-permute-start | bytes 786440 | tf_op jit(solution)/shard_map/ppermute | solution.py:423
  22.1 7.8 %collective-permute-start.3 = (f32[2,128,256]{2,1,0:T(8,128)S(1)}, f32[2,128,256]{2,1,0:T(8,128)S(1)}, u32[]{:S(2)}, u32[]{:S(2)}) collective-permute-start(f32[2,128,256]{2,1,0:T(8,128)S(1)} %collective-permute-done.2.refs_0_), channel_id=1, source_target_pairs={{0,8},{8,0},{1,9},{9,1},{2,10},{10,2},{3,11},{11,3},{4,12},{12,4},... | collective-permute-start | bytes 786440 | tf_op jit(solution)/shard_map/ppermute | solution.py:423
  31.7 10.2 %copy-start.3 = (f32[4,256,256]{2,1,0:T(8,128)S(1)}, f32[4,256,256]{2,1,0:T(8,128)}, u32[]{:S(2)}) copy-start(f32[4,256,256]{2,1,0:T(8,128)} %measured.1) | copy-start | bytes 3145732
  37.9 10.4 %collective-permute-start.8 = (f32[256,256]{1,0:T(8,128)S(1)}, f32[256,256]{1,0:T(8,128)S(1)}, u32[]{:S(2)}, u32[]{:S(2)}) collective-permute-start(f32[256,256]{1,0:T(8,128)S(1)} %get-tuple-element.41.power), channel_id=1, source_target_pairs={{0,1},{1,0},{2,3},{3,2},{4,5},{5,4},{6,7},{7,6},{8,9},{9,8},{10,11... | collective-permute-start | bytes 786440 | tf_op jit(solution)/shard_map/ppermute | solution.py:475
  60.5 2.9 %collective-permute-start.24 = (f32[8,4,2,16,256]{4,3,2,1,0:T(8,128)S(1)}, f32[8,4,2,16,256]{4,3,2,1,0:T(8,128)S(1)}, u32[]{:S(2)}, u32[]{:S(2)}) collective-permute-start(f32[8,4,2,16,256]{4,3,2,1,0:T(8,128)S(1)} %get-tuple-element.53), channel_id=1, source_target_pairs={{0,8},{8,0},{1,9},{9,1},{2,10},{10,2},{3,11},{11,3},{4,12},{12,4},... | collective-permute-start | bytes 3145736 | tf_op jit(solution)/shard_map/ppermute | solution.py:493
  64.6 44.4 %all-to-all-start = ((f32[32,2,16,256]{3,2,1,0:T(8,128)}), f32[32,2,16,256]{3,2,1,0:T(8,128)S(1)}, u32[]{:S(2)}, u32[]{:S(2)}) async-start(f32[32,2,16,256]{3,2,1,0:T(8,128)} %bitcast.3), calls=%async_computation | async-start | bytes 2097152 | tf_op jit(solution)/shard_map/all_to_all | solution.py:498
  72.8 18.3 %collective-permute-start.10 = (f32[2,2,32,256]{3,2,1,0:T(8,128)S(1)}, f32[2,2,32,256]{3,2,1,0:T(8,128)S(1)}, u32[]{:S(2)}, u32[]{:S(2)}) collective-permute-start(f32[2,2,32,256]{3,2,1,0:T(8,128)S(1)} %get-tuple-element.44), channel_id=1, source_target_pairs={{0,2},{1,3},{2,4},{3,5},{4,6},{5,7},{6,0},{7,1},{8,10},{9,11},{10,... | collective-permute-start | bytes 393224 | tf_op jit(solution)/shard_map/ppermute | solution.py:496
  74.7 23.6 %collective-permute-start.11 = (f32[2,2,32,256]{3,2,1,0:T(8,128)S(1)}, f32[2,2,32,256]{3,2,1,0:T(8,128)S(1)}, u32[]{:S(2)}, u32[]{:S(2)}) collective-permute-start(f32[2,2,32,256]{3,2,1,0:T(8,128)S(1)} %get-tuple-element.45), channel_id=1, source_target_pairs={{0,3},{1,4},{2,5},{3,6},{4,7},{5,0},{6,1},{7,2},{8,11},{9,12},{10,... | collective-permute-start | bytes 393224 | tf_op jit(solution)/shard_map/ppermute | solution.py:496
  79.1 19.1 %collective-permute-start.12 = (f32[2,2,32,256]{3,2,1,0:T(8,128)S(1)}, f32[2,2,32,256]{3,2,1,0:T(8,128)S(1)}, u32[]{:S(2)}, u32[]{:S(2)}) collective-permute-start(f32[2,2,32,256]{3,2,1,0:T(8,128)S(1)} %get-tuple-element.46), channel_id=1, source_target_pairs={{0,4},{1,5},{2,6},{3,7},{4,0},{5,1},{6,2},{7,3},{8,12},{9,13},{10,... | collective-permute-start | bytes 393224 | tf_op jit(solution)/shard_map/ppermute | solution.py:496
  80.6 18.7 %collective-permute-start.13 = (f32[2,2,32,256]{3,2,1,0:T(8,128)S(1)}, f32[2,2,32,256]{3,2,1,0:T(8,128)S(1)}, u32[]{:S(2)}, u32[]{:S(2)}) collective-permute-start(f32[2,2,32,256]{3,2,1,0:T(8,128)S(1)} %get-tuple-element.47), channel_id=1, source_target_pairs={{0,5},{1,6},{2,7},{3,0},{4,1},{5,2},{6,3},{7,4},{8,13},{9,14},{10,... | collective-permute-start | bytes 393224 | tf_op jit(solution)/shard_map/ppermute | solution.py:496
  83.3 16.1 %collective-permute-start.14 = (f32[2,2,32,256]{3,2,1,0:T(8,128)S(1)}, f32[2,2,32,256]{3,2,1,0:T(8,128)S(1)}, u32[]{:S(2)}, u32[]{:S(2)}) collective-permute-start(f32[2,2,32,256]{3,2,1,0:T(8,128)S(1)} %get-tuple-element.48), channel_id=1, source_target_pairs={{0,6},{1,7},{2,0},{3,1},{4,2},{5,3},{6,4},{7,5},{8,14},{9,15},{10,... | collective-permute-start | bytes 393224 | tf_op jit(solution)/shard_map/ppermute | solution.py:496
  91.1 10.4 %collective-permute-start.15 = (f32[2,2,32,256]{3,2,1,0:T(8,128)S(1)}, f32[2,2,32,256]{3,2,1,0:T(8,128)S(1)}, u32[]{:S(2)}, u32[]{:S(2)}) collective-permute-start(f32[2,2,32,256]{3,2,1,0:T(8,128)S(1)} %get-tuple-element.49), channel_id=1, source_target_pairs={{0,7},{1,0},{2,1},{3,2},{4,3},{5,4},{6,5},{7,6},{8,15},{9,8},{10,9... | collective-permute-start | bytes 393224 | tf_op jit(solution)/shard_map/ppermute | solution.py:496
  98.2 8.6 %collective-permute-start.9 = (f32[2,2,32,256]{3,2,1,0:T(8,128)S(1)}, f32[2,2,32,256]{3,2,1,0:T(8,128)S(1)}, u32[]{:S(2)}, u32[]{:S(2)}) collective-permute-start(f32[2,2,32,256]{3,2,1,0:T(8,128)S(1)} %get-tuple-element.43), channel_id=1, source_target_pairs={{0,1},{1,2},{2,3},{3,4},{4,5},{5,6},{6,7},{7,0},{8,9},{9,10},{10,1... | collective-permute-start | bytes 393224 | tf_op jit(solution)/shard_map/ppermute | solution.py:496
  107.7 8.3 %collective-permute-start.16 = (f32[2,2,32,384]{3,2,1,0:T(8,128)S(1)}, f32[2,2,32,384]{3,2,1,0:T(8,128)S(1)}, u32[]{:S(2)}, u32[]{:S(2)}) collective-permute-start(f32[2,2,32,384]{3,2,1,0:T(8,128)S(1)} %get-tuple-element.51), channel_id=1, source_target_pairs={{0,8},{8,16},{16,24},{24,32},{32,40},{40,48},{48,56},{56,64},{64,7... | collective-permute-start | bytes 589832 | tf_op jit(solution)/shard_map/ppermute | solution.py:508
  109.9 37.2 %all-to-all-start.1 = ((f32[16,2,16,256]{3,2,1,0:T(8,128)}), f32[16,2,16,256]{3,2,1,0:T(8,128)S(1)}, u32[]{:S(2)}, u32[]{:S(2)}) async-start(f32[16,2,16,256]{3,2,1,0:T(8,128)} %broadcast_in_dim.3), calls=%async_computation.1 | async-start | bytes 1048576 | tf_op jit(solution)/shard_map/all_to_all | solution.py:514
  116.1 15.0 %collective-permute-start.17 = (f32[2,2,32,384]{3,2,1,0:T(8,128)S(1)}, f32[2,2,32,384]{3,2,1,0:T(8,128)S(1)}, u32[]{:S(2)}, u32[]{:S(2)}) collective-permute-start(f32[2,2,32,384]{3,2,1,0:T(8,128)S(1)} %add.6.refs_0_), channel_id=1, source_target_pairs={{0,1},{1,2},{2,3},{3,4},{4,5},{5,6},{6,7},{7,0},{8,9},{9,10},{10,1... | collective-permute-start | bytes 589832 | tf_op jit(solution)/shard_map/ppermute | solution.py:513
  116.9 19.2 %collective-permute-start.18 = (f32[2,2,32,384]{3,2,1,0:T(8,128)S(1)}, f32[2,2,32,384]{3,2,1,0:T(8,128)S(1)}, u32[]{:S(2)}, u32[]{:S(2)}) collective-permute-start(f32[2,2,32,384]{3,2,1,0:T(8,128)S(1)} %add.6.refs_0_), channel_id=1, source_target_pairs={{0,2},{1,3},{2,4},{3,5},{4,6},{5,7},{6,0},{7,1},{8,10},{9,11},{10,... | collective-permute-start | bytes 589832 | tf_op jit(solution)/shard_map/ppermute | solution.py:513
  116.9 23.9 %collective-permute-start.19 = (f32[2,2,32,384]{3,2,1,0:T(8,128)S(1)}, f32[2,2,32,384]{3,2,1,0:T(8,128)S(1)}, u32[]{:S(2)}, u32[]{:S(2)}) collective-permute-start(f32[2,2,32,384]{3,2,1,0:T(8,128)S(1)} %add.6.refs_0_), channel_id=1, source_target_pairs={{0,3},{1,4},{2,5},{3,6},{4,7},{5,0},{6,1},{7,2},{8,11},{9,12},{10,... | collective-permute-start | bytes 589832 | tf_op jit(solution)/shard_map/ppermute | solution.py:513
  120.7 20.1 %collective-permute-start.20 = (f32[2,2,32,384]{3,2,1,0:T(8,128)S(1)}, f32[2,2,32,384]{3,2,1,0:T(8,128)S(1)}, u32[]{:S(2)}, u32[]{:S(2)}) collective-permute-start(f32[2,2,32,384]{3,2,1,0:T(8,128)S(1)} %add.6.refs_0_), channel_id=1, source_target_pairs={{0,4},{1,5},{2,6},{3,7},{4,0},{5,1},{6,2},{7,3},{8,12},{9,13},{10,... | collective-permute-start | bytes 589832 | tf_op jit(solution)/shard_map/ppermute | solution.py:513
  123.2 18.0 %collective-permute-start.21 = (f32[2,2,32,384]{3,2,1,0:T(8,128)S(1)}, f32[2,2,32,384]{3,2,1,0:T(8,128)S(1)}, u32[]{:S(2)}, u32[]{:S(2)}) collective-permute-start(f32[2,2,32,384]{3,2,1,0:T(8,128)S(1)} %add.6.refs_0_), channel_id=1, source_target_pairs={{0,5},{1,6},{2,7},{3,0},{4,1},{5,2},{6,3},{7,4},{8,13},{9,14},{10,... | collective-permute-start | bytes 589832 | tf_op jit(solution)/shard_map/ppermute | solution.py:513
  131.1 10.2 %collective-permute-start.22 = (f32[2,2,32,384]{3,2,1,0:T(8,128)S(1)}, f32[2,2,32,384]{3,2,1,0:T(8,128)S(1)}, u32[]{:S(2)}, u32[]{:S(2)}) collective-permute-start(f32[2,2,32,384]{3,2,1,0:T(8,128)S(1)} %add.6.refs_0_), channel_id=1, source_target_pairs={{0,6},{1,7},{2,0},{3,1},{4,2},{5,3},{6,4},{7,5},{8,14},{9,15},{10,... | collective-permute-start | bytes 589832 | tf_op jit(solution)/shard_map/ppermute | solution.py:513
  136.0 9.4 %collective-permute-start.23 = (f32[2,2,32,384]{3,2,1,0:T(8,128)S(1)}, f32[2,2,32,384]{3,2,1,0:T(8,128)S(1)}, u32[]{:S(2)}, u32[]{:S(2)}) collective-permute-start(f32[2,2,32,384]{3,2,1,0:T(8,128)S(1)} %add.6.refs_0_), channel_id=1, source_target_pairs={{0,7},{1,0},{2,1},{3,2},{4,3},{5,4},{6,5},{7,6},{8,15},{9,8},{10,9... | collective-permute-start | bytes 589832 | tf_op jit(solution)/shard_map/ppermute | solution.py:513

commit v2 on v1

--- a/solution.py
+++ b/solution.py
@@ -181,19 +181,22 @@
         copy.wait()
 
 
-def spread_mode(pair, window, prop, tables, lane, row_table, mid, out):
+def spread_modes(pairs, window, prop, tables, lane, row_table, mid, out):
     for rows in BLOCKS:
-        real, imag = pair(rows)
-        real, imag = times(real, imag, window[0, rows, :], window[1, rows, :])
-        real, imag = right_forward(real, imag, tables, lane)
-        mid[0, rows, :] = real
-        mid[1, rows, :] = imag
+        for mode, pair in enumerate(pairs):
+            real, imag = pair(rows)
+            real, imag = times(real, imag, window[0, rows, :], window[1, rows, :])
+            real, imag = right_forward(real, imag, tables, lane)
+            mid[mode, 0, rows, :] = real
+            mid[mode, 1, rows, :] = imag
     for cols in BLOCKS:
-        real, imag = left_forward(mid[0, :, cols], mid[1, :, cols], tables, row_table)
-        real, imag = times(prop[0, :, cols], prop[1, :, cols], real, imag)
-        real, imag = left_inverse(real, imag, tables, row_table)
-        out[0, :, cols] = real
-        out[1, :, cols] = imag
+        for mode in range(len(pairs)):
+            real, imag = left_forward(mid[mode, 0, :, cols], mid[mode, 1, :, cols], tables,
+                                      row_table)
+            real, imag = times(prop[0, :, cols], prop[1, :, cols], real, imag)
+            real, imag = left_inverse(real, imag, tables, row_table)
+            out[mode, 0, :, cols] = real
+            out[mode, 1, :, cols] = imag
 
 
 def start_kernel(place, row_off, col_off, own, halo, probe, prop, tables, lane, row_table,
@@ -201,52 +204,63 @@
     slot = place[0]
     cut_window(own, halo, row_off[slot], col_off[slot], window)
     probes[0] = probe[0]
-    spread_mode(lambda rows: (probe[0, 0, rows, :], probe[0, 1, rows, :]), window, prop, tables,
-                lane, row_table, mid, moved.at[0])
+    spread_modes([lambda rows: (probe[0, 0, rows, :], probe[0, 1, rows, :])], window, prop, tables,
+                 lane, row_table, mid, moved)
 
 
 def first_kernel(count, place, window, *refs):
     mine, other = refs[:count], refs[count : 2 * count]
     prop, tables, lane, row_table, _, _, moved, probes, mid = refs[2 * count :]
-    core, step = place[2], pl.program_id(0)
-
-    def pair(rows):
-        index = BLOCKS.index(rows)
-        values = []
-        for part in range(2):
-            value = jnp.where(core == index, mine[0][part], other[0][part])
-            if count == 2:
-                later = jnp.where(core == index, mine[1][part], other[1][part])
-                value = jnp.where(step == 0, value, later)
-            probes[0, part, rows, :] = value
-            values.append(value)
-        return values
-
-    spread_mode(pair, window, prop, tables, lane, row_table, mid, moved.at[0])
+    core = place[2]
+
+    def source(mode):
+        def pair(rows):
+            index = BLOCKS.index(rows)
+            values = []
+            for part in range(2):
+                value = jnp.where(core == index, mine[mode][part], other[mode][part])
+                probes[mode, part, rows, :] = value
+                values.append(value)
+            return values
+
+        return pair
+
+    spread_modes([source(mode) for mode in range(count)], window, prop, tables, lane, row_table,
+                 mid, moved)
+
+
+GROUP = 4
 
 
 def second_kernel(place, row_off, col_off, own, halo, moved, tables, lane, row_table,
                   before, far, power, window, mid):
     slot = place[0]
-
-    @pl.when(pl.program_id(0) == 0)
-    def _():
-        cut_window(own, halo, row_off[slot], col_off[slot], window)
-        power[...] = jnp.zeros(power.shape, F32)
-
-    for rows in BLOCKS:
-        real, imag = right_inverse(moved[0, 0, rows, :], moved[0, 1, rows, :], tables, lane)
-        before[0, 0, rows, :] = real
-        before[0, 1, rows, :] = imag
-        real, imag = times(real, imag, window[0, rows, :], window[1, rows, :])
-        real, imag = right_forward(real, imag, tables, lane)
-        mid[0, rows, :] = real
-        mid[1, rows, :] = imag
-    for cols in BLOCKS:
-        real, imag = left_forward(mid[0, :, cols], mid[1, :, cols], tables, row_table)
-        far[0, 0, :, cols] = real
-        far[0, 1, :, cols] = imag
-        power[:, cols] += real * real + imag * imag
+    cut_window(own, halo, row_off[slot], col_off[slot], window)
+    power[...] = jnp.zeros(power.shape, F32)
+
+    def some_modes(base, carry):
+        for rows in BLOCKS:
+            for m in range(GROUP):
+                mode = GROUP * base + m
+                real, imag = right_inverse(
+                    moved[mode, 0, rows, :], moved[mode, 1, rows, :], tables, lane
+                )
+                before[mode, 0, rows, :] = real
+                before[mode, 1, rows, :] = imag
+                real, imag = times(real, imag, window[0, rows, :], window[1, rows, :])
+                real, imag = right_forward(real, imag, tables, lane)
+                mid[m, 0, rows, :] = real
+                mid[m, 1, rows, :] = imag
+        for cols in BLOCKS:
+            for m in range(GROUP):
+                mode = GROUP * base + m
+                real, imag = left_forward(mid[m, 0, :, cols], mid[m, 1, :, cols], tables, row_table)
+                far[mode, 0, :, cols] = real
+                far[mode, 1, :, cols] = imag
+                power[:, cols] += real * real + imag * imag
+        return carry
+
+    some_modes(0, 0)
 
 
 def third_kernel(place, row_off, col_off, counts, far, before, window0, window1, probes, prop,
@@ -254,60 +268,68 @@
                  *rest):
     pieces, (keep, send, weight, mid, late, terms) = rest[:8], rest[8:]
     slot, core = place[0], place[2]
-
-    @pl.when(pl.program_id(0) == 0)
-    def _():
-        alive = jnp.where(slot < counts[0], 1.0 / MODES, 0.0).astype(F32)
-        weight[...] = (power[...] + power_other[...] - measured[...]) * alive
-        terms[...] = jnp.zeros(terms.shape, F32)
-
-    for cols in BLOCKS:
-        scale = weight[:, cols]
-        real, imag = left_inverse(
-            far[0, 0, :, cols] * scale, far[0, 1, :, cols] * scale, tables, row_table
-        )
-        mid[0, :, cols] = real
-        mid[1, :, cols] = imag
-    for rows in BLOCKS:
-        real, imag = right_inverse(mid[0, rows, :], mid[1, rows, :], tables, lane)
-        tr, ti = times_conj(before[0, 0, rows, :], before[0, 1, rows, :], real, imag)
-        terms[1, 0, rows, :] += tr
-        terms[1, 1, rows, :] += ti
-        real, imag = times_conj(window1[0, rows, :], window1[1, rows, :], real, imag)
-        real, imag = right_forward(real, imag, tables, lane)
-        late[0, rows, :] = real
-        late[1, rows, :] = imag
-    for cols in BLOCKS:
-        real, imag = left_forward(late[0, :, cols], late[1, :, cols], tables, row_table)
-        real, imag = times_conj(prop[0, :, cols], prop[1, :, cols], real, imag)
-        real, imag = left_inverse(real, imag, tables, row_table)
-        mid[0, :, cols] = real
-        mid[1, :, cols] = imag
-    for index, rows in enumerate(BLOCKS):
-        real, imag = right_inverse(mid[0, rows, :], mid[1, rows, :], tables, lane)
-        tr, ti = times_conj(probes[0, 0, rows, :], probes[0, 1, rows, :], real, imag)
-        terms[0, 0, rows, :] += tr
-        terms[0, 1, rows, :] += ti
-        pair = times_conj(window0[0, rows, :], window0[1, rows, :], real, imag)
+    alive = jnp.where(slot < counts[0], 1.0 / MODES, 0.0).astype(F32)
+    weight[...] = (power[...] + power_other[...] - measured[...]) * alive
+    terms[...] = jnp.zeros(terms.shape, F32)
+
+    def some_modes(base, carry):
+        for cols in BLOCKS:
+            scale = weight[:, cols]
+            for m in range(GROUP):
+                mode = GROUP * base + m
+                real, imag = left_inverse(
+                    far[mode, 0, :, cols] * scale, far[mode, 1, :, cols] * scale, tables, row_table
+                )
+                mid[m, 0, :, cols] = real
+                mid[m, 1, :, cols] = imag
+        for rows in BLOCKS:
+            for m in range(GROUP):
+                mode = GROUP * base + m
+                real, imag = right_inverse(mid[m, 0, rows, :], mid[m, 1, rows, :], tables, lane)
+                tr, ti = times_conj(before[mode, 0, rows, :], before[mode, 1, rows, :], real, imag)
+                terms[1, 0, rows, :] += tr
+                terms[1, 1, rows, :] += ti
+                real, imag = times_conj(window1[0, rows, :], window1[1, rows, :], real, imag)
+                real, imag = right_forward(real, imag, tables, lane)
+                late[m, 0, rows, :] = real
+                late[m, 1, rows, :] = imag
+        for cols in BLOCKS:
+            for m in range(GROUP):
+                real, imag = left_forward(late[m, 0, :, cols], late[m, 1, :, cols], tables,
+                                          row_table)
+                real, imag = times_conj(prop[0, :, cols], prop[1, :, cols], real, imag)
+                real, imag = left_inverse(real, imag, tables, row_table)
+                mid[m, 0, :, cols] = real
+                mid[m, 1, :, cols] = imag
+        for index, rows in enumerate(BLOCKS):
+            for m in range(GROUP):
+                mode = GROUP * base + m
+                step = jnp.where(mode < 2, 2 * mode + 1, 2 * mode - 4)
+                home = lax.rem(slot - step + 4, 4)
+                real, imag = right_inverse(mid[m, 0, rows, :], mid[m, 1, rows, :], tables, lane)
+                tr, ti = times_conj(probes[mode, 0, rows, :], probes[mode, 1, rows, :], real, imag)
+                terms[0, 0, rows, :] += tr
+                terms[0, 1, rows, :] += ti
+                pair = times_conj(window0[0, rows, :], window0[1, rows, :], real, imag)
+                for part in range(2):
+                    for group in range(4):
+                        upper = pair[part][group * 32 : group * 32 + 16]
+                        lower = pair[part][group * 32 + 16 : group * 32 + 32]
+                        keep[index * 4 + group, home, part] = jnp.where(core == 0, upper, lower)
+                        send[index * 4 + group, home, part] = jnp.where(core == 0, lower, upper)
+        return carry
+
+    some_modes(0, 0)
+    for layer in range(2):
         for part in range(2):
-            for group in range(4):
-                upper = pair[part][group * 32 : group * 32 + 16]
-                lower = pair[part][group * 32 + 16 : group * 32 + 32]
-                keep[index * 4 + group, 0, part] = jnp.where(core == 0, upper, lower)
-                send[index * 4 + group, 0, part] = jnp.where(core == 0, lower, upper)
-
-    @pl.when(pl.program_id(0) == 3)
-    def _():
+            ring = pltpu.roll(terms[layer, part], row_off[slot], 0)
+            terms[layer, part] = pltpu.roll(ring, col_off[slot], 1)
+    shard = place[0] * 2 + place[1]
+    for step in range(8):
+        start = pl.multiple_of(lax.rem(shard + step, 8) * 32, 32)
         for layer in range(2):
             for part in range(2):
-                ring = pltpu.roll(terms[layer, part], row_off[slot], 0)
-                terms[layer, part] = pltpu.roll(ring, col_off[slot], 1)
-        shard = place[0] * 2 + place[1]
-        for step in range(8):
-            start = pl.multiple_of(lax.rem(shard + step, 8) * 32, 32)
-            for layer in range(2):
-                for part in range(2):
-                    pieces[step][layer, part] = terms[layer, part, pl.ds(start, 32), :]
+                pieces[step][layer, part] = terms[layer, part, pl.ds(start, 32), :]
 
 
 def gather_kernel(place, row_off, col_off, *refs):
@@ -333,16 +355,20 @@
             halo[layer, part] = jnp.concatenate(next_one, axis=1)
 
 
-def join_kernel(first, last, place, *refs):
+def total_kernel(spread, out):
+    value = jnp.sum(spread[...], axis=0)
+    for k in range(16):
+        out[k] = value
+
+
+def join_kernel(place, *refs):
     out, sem = refs[-2], refs[-1]
     shard = place[0] * 2 + place[1]
     copies = []
-    for step in range(first, last):
+    for step in range(8):
         start = pl.multiple_of(lax.rem(shard - step + 8, 8) * 32, 32)
         copies.append(
-            pltpu.make_async_copy(
-                refs[step - first], out.at[:, :, pl.ds(start, 32), :], sem.at[step]
-            )
+            pltpu.make_async_copy(refs[step], out.at[:, :, pl.ds(start, 32), :], sem.at[step])
         )
     for copy in copies:
         copy.start()
@@ -354,21 +380,9 @@
     return pl.BlockSpec(sizes, lambda *_: (0,) * len(sizes))
 
 
-def by_mode(*sizes):
-    return pl.BlockSpec((1,) + sizes, lambda i, *_: (i,) + (0,) * len(sizes))
-
-
-def by_home():
-    return pl.BlockSpec(
-        (8, 1, 2, 16, WIN), lambda i, place, *_: (0, lax.rem(place[0] - i + 4, 4), 0, 0, 0)
-    )
-
-
 TABLES = [VMEM, VMEM, VMEM]
 PLANE = whole(WIN, WIN)
 FIELD = whole(2, WIN, WIN)
-MODAL = by_mode(2, WIN, WIN)
-STRIP = whole(2, WIN, COLS)
 
 
 ANY = pl.BlockSpec(memory_space=pl.ANY)
@@ -445,48 +459,50 @@
 
     modes = shape(4, 2, WIN, WIN)
     tables = (matrices, lane_table, row_table)
-    work = [pltpu.VMEM((2, WIN, WIN), F32)]
+
+    def work(count):
+        return [pltpu.VMEM((count, 2, WIN, WIN), F32)]
+
+    def block(size, index):
+        return pl.BlockSpec((size, 2, WIN, WIN), lambda *_: (index, 0, 0, 0))
+
     moved, probes, window0 = modal_call(
         start_kernel, 3, 1,
-        [STRIP, STRIP, MODAL, FIELD] + TABLES,
-        [MODAL, MODAL, FIELD], (modes, modes, shape(2, WIN, WIN)), work,
+        [VMEM] * 4 + TABLES,
+        [block(1, 2), block(1, 2), FIELD], (modes, modes, shape(2, WIN, WIN)), work(1),
     )(place, row_offset, col_offset, layer0, halo0, probe, prop, *tables)
-    for steps in ((1, 3), (2,)):
+    for steps, index in (((1, 3), 0), ((2,), 3)):
         count = len(steps)
-        target_block = pl.BlockSpec(
-            (1, 2, WIN, WIN), lambda i, *_, base=steps[0]: (base + 2 * i, 0, 0, 0)
-        )
         moved, probes = modal_call(
-            functools.partial(first_kernel, count), 1, count,
+            functools.partial(first_kernel, count), 1, 1,
             [VMEM] * (2 * count + 2) + TABLES + [ANY, ANY],
-            [target_block, target_block], (modes, modes), work,
+            [block(count, index)] * 2, (modes, modes), work(count),
             {2 * count + 6: 0, 2 * count + 7: 1},
         )(place, window0, *[mine[k] for k in steps], *[other[k] for k in steps], prop,
           *tables, moved, probes)
 
-    before, far, power, window1 = modal_call(
-        second_kernel, 3, 4,
-        [STRIP, STRIP, MODAL] + TABLES,
-        [MODAL, MODAL, PLANE, FIELD],
-        (modes, modes, shape(WIN, WIN), shape(2, WIN, WIN)),
-        work,
+    before, far, power, window1 = pl.pallas_call(
+        second_kernel,
+        in_specs=[SMEM] * 3 + [VMEM] * 6,
+        out_specs=[VMEM] * 4,
+        out_shape=(modes, modes, shape(WIN, WIN), shape(2, WIN, WIN)),
+        scratch_shapes=work(GROUP),
+        compiler_params=PARAMS,
+        name="second",
     )(place, row_offset, col_offset, layer1, halo1, moved, *tables)
 
     power_other = lax.ppermute(power, "zh", [(0, 1), (1, 0)])
 
     parts_shape = shape(8, 4, 2, 16, WIN)
     piece = shape(2, 2, 32, WIN)
-    *pieces, keep, send = modal_call(
-        third_kernel, 4, 4,
-        [MODAL, MODAL, VMEM, VMEM, MODAL] + [VMEM] * 4 + TABLES,
-        [whole(2, 2, 32, WIN)] * 8 + [by_home(), by_home()],
-        (piece,) * 8 + (parts_shape, parts_shape),
-        [
-            pltpu.VMEM((WIN, WIN), F32),
-            pltpu.VMEM((2, WIN, WIN), F32),
-            pltpu.VMEM((2, WIN, WIN), F32),
-            pltpu.VMEM((2, 2, WIN, WIN), F32),
-        ],
+    *pieces, keep, send = pl.pallas_call(
+        third_kernel,
+        in_specs=[SMEM] * 4 + [VMEM] * 12,
+        out_specs=[VMEM] * 10,
+        out_shape=(piece,) * 8 + (parts_shape, parts_shape),
+        scratch_shapes=[pltpu.VMEM((WIN, WIN), F32)] + work(GROUP) * 3,
+        compiler_params=PARAMS,
+        name="third",
     )(place, row_offset, col_offset, counts, far, before, window0, window1, probes, prop, power,
       power_other, target, *tables)
 
@@ -496,7 +512,6 @@
         arrived.append(lax.ppermute(pieces[k], MODE, ring_route(8, k)))
     kept = keep + swapped
     spread = lax.all_to_all(kept.reshape(32, 2, 16, WIN), SPREAD, 0, 0)
-    probe_part = jnp.sum(spread, axis=0)
     own, over = pl.pallas_call(
         gather_kernel,
         out_shape=(shape(2, 2, 32, COLS), shape(2, 2, 32, COLS)),
@@ -508,29 +523,27 @@
     over_in = lax.ppermute(over, TILE, ahead)
 
     total = own + over_in
-    parts = []
+    parts = [total]
     for k in range(1, 8):
         parts.append(lax.ppermute(total, MODE, ring_route(8, k)))
-    probe_all = lax.all_to_all(jnp.broadcast_to(probe_part, (16, 2, 16, WIN)), TILE, 0, 0)
+    probe_part = pl.pallas_call(
+        total_kernel,
+        in_specs=[VMEM],
+        out_specs=VMEM,
+        out_shape=shape(16, 2, 16, WIN),
+        compiler_params=PARAMS,
+        name="psum",
+    )(spread)
+    probe_all = lax.all_to_all(probe_part, TILE, 0, 0)
     object_grad = pl.pallas_call(
-        functools.partial(join_kernel, 0, 1),
+        join_kernel,
         out_shape=shape(2, 2, WIN, COLS),
-        in_specs=[SMEM, VMEM],
+        in_specs=[SMEM] + [VMEM] * 8,
         out_specs=ANY,
         scratch_shapes=[pltpu.SemaphoreType.DMA((8,))],
         compiler_params=PARAMS,
-        name="joina",
-    )(place, total)
-    object_grad = pl.pallas_call(
-        functools.partial(join_kernel, 1, 8),
-        out_shape=shape(2, 2, WIN, COLS),
-        in_specs=[SMEM] + [VMEM] * 7 + [ANY],
-        out_specs=ANY,
-        scratch_shapes=[pltpu.SemaphoreType.DMA((8,))],
-        input_output_aliases={8: 0},
-        compiler_params=PARAMS,
-        name="joinb",
-    )(place, *parts, object_grad)
+        name="join",
+    )(place, *parts)
     probe_grad = jnp.transpose(probe_all, (1, 0, 2, 3)).reshape(1, 2, WIN, WIN)
     return object_grad, probe_grad
 

time: 149 us -> 142 us (0.953)
  Pallas kernels: 34.2 us -> 26.8 us
    pallas_call x7, Pallas kernels: 28.7 us -> 21.3 us  [the longest x1 7.65 us: per_device(): pl.pallas_call(third_kernel, in_specs=[SMEM] * 4 + [VMEM] * 12, out_specs...]
  transfers between devices with their start and end apart: 27 -> 27, of which waited for: 13 -> 14; matrix products, arithmetic and copies ran while one was open for 1% -> 0% of each run, Pallas kernels for 9% -> 9%
where the time goes in v2:
time: 142 us; the launch traced here: 141 us
  starting transfers between devices  63.7 us (45%)
  waiting for transfers between devices  46.6 us (33%)
  Pallas kernels  26.8 us (19%)
  between operations  1.62 us (1%)
    ppermute x7, waiting for transfers between devices, per_device(): arrived.append(lax.ppermute(pieces[k], MODE, ring_route(8, k)))  18 us
    ppermute x7, starting transfers between devices, per_device(): parts.append(lax.ppermute(total, MODE, ring_route(8, k)))  17.4 us
    ppermute x7, starting transfers between devices, per_device(): arrived.append(lax.ppermute(pieces[k], MODE, ring_route(8, k)))  16 us
    ppermute x7, waiting for transfers between devices, per_device(): parts.append(lax.ppermute(total, MODE, ring_route(8, k)))  12 us
    ppermute x3, waiting for transfers between devices, per_device(): mine[k] = lax.ppermute(half, 'y', ring_route(4, k))  9.33 us
    all_to_all x1, starting transfers between devices, per_device(): spread = lax.all_to_all(kept.reshape(32, 2, 16, WIN), SPREAD, 0, 0)  8.23 us
    pallas_call x1, Pallas kernels, per_device(): pl.pallas_call(third_kernel, in_specs=[SMEM] * 4 + [VMEM] * 12, out_specs...  7.65 us
    all_to_all x1, starting transfers between devices, per_device(): probe_all = lax.all_to_all(probe_part, TILE, 0, 0)  6.05 us
  transfers between devices with their start and end apart: 27, of which 14 were waited for; matrix products, arithmetic and copies ran while one was open for 0% of the time, Pallas kernels for 9%

profile of v2, /device:TPU:0, one launch (start us, length us, event | category | flops | bytes accessed | tf_op | source)
XLA Modules:
  0.0 140.9 jit_solution(13777275365939111566)
XLA Ops:
  0.6 0.0 copy-start.4
  0.6 0.0 copy-start
  0.7 0.0 copy-start.6
  0.7 0.0 copy-start.1
  0.7 0.0 copy-start.2
  0.7 0.1 pad_add_fusion.place
  0.8 2.0 %cut.1 = (f32[2,256,384]{2,1,0:T(8,128)S(1)}, f32[2,256,384]{2,1,0:T(8,128)S(1)}, f32[2,128,256]{2,1,0:T(8,128)S(1)}) custom-call(s32[3]{0:T(128)S(1)} %pad_add_fusion.place, f32[2,2,256,384]{3,2,1,0:T(8,128)} %field.1, f32[1,2,256,256]{3,2,1,0:T(8,128)} %probe.3), custom_call_target="tpu_custom_call" | custom-call | tf_op jit(solution)/shard_map/cut/pallas_call | solution.py:422
  2.8 1.3 collective-permute-start.1
  4.1 1.3 collective-permute-start
  5.4 1.8 %collective-permute-start.4 = (f32[2,128,256]{2,1,0:T(8,128)S(1)}, f32[2,128,256]{2,1,0:T(8,128)S(1)}, u32[]{:S(2)}, u32[]{:S(2)}) collective-permute-start(f32[2,128,256]{2,1,0:T(8,128)S(1)} %get-tuple-element.31), channel_id=1, source_target_pairs={{0,2},{2,4},{4,6},{6,0},{1,3},{3,5},{5,7},{7,1},{8,10},{10,12},{12... | collective-permute-start | bytes 786440 | tf_op jit(solution)/shard_map/ppermute | solution.py:436
  7.2 1.5 %collective-permute-start.5 = (f32[2,128,256]{2,1,0:T(8,128)S(1)}, f32[2,128,256]{2,1,0:T(8,128)S(1)}, u32[]{:S(2)}, u32[]{:S(2)}) collective-permute-start(f32[2,128,256]{2,1,0:T(8,128)S(1)} %get-tuple-element.31), channel_id=1, source_target_pairs={{0,6},{2,0},{4,2},{6,4},{1,7},{3,1},{5,3},{7,5},{8,14},{10,8},{12,... | collective-permute-start | bytes 786440 | tf_op jit(solution)/shard_map/ppermute | solution.py:436
  8.7 2.1 %collective-permute-start.2 = (f32[2,128,256]{2,1,0:T(8,128)S(1)}, f32[2,128,256]{2,1,0:T(8,128)S(1)}, u32[]{:S(2)}, u32[]{:S(2)}) collective-permute-start(f32[2,128,256]{2,1,0:T(8,128)S(1)} %get-tuple-element.31), channel_id=1, source_target_pairs={{0,4},{2,6},{4,0},{6,2},{1,5},{3,7},{5,1},{7,3},{8,12},{10,14},{12... | collective-permute-start | bytes 786440 | tf_op jit(solution)/shard_map/ppermute | solution.py:436
  10.8 4.1 %collective-permute-done.4.refs_0_ = f32[2,128,256]{2,1,0:T(8,128)S(1)} collective-permute-done((f32[2,128,256]{2,1,0:T(8,128)S(1)}, f32[2,128,256]{2,1,0:T(8,128)S(1)}, u32[]{:S(2)}, u32[]{:S(2)}) %collective-permute-start.4) | collective-permute-done | bytes 262176 | tf_op jit(solution)/shard_map/ppermute | solution.py:436
  14.9 0.8 collective-permute-start.6
  15.7 0.1 collective-permute-done.5.refs_1_
  15.9 1.1 collective-permute-start.7
  17.0 5.1 %collective-permute-done.2.refs_0_ = f32[2,128,256]{2,1,0:T(8,128)S(1)} collective-permute-done((f32[2,128,256]{2,1,0:T(8,128)S(1)}, f32[2,128,256]{2,1,0:T(8,128)S(1)}, u32[]{:S(2)}, u32[]{:S(2)}) %collective-permute-start.2) | collective-permute-done | bytes 262176 | tf_op jit(solution)/shard_map/ppermute | solution.py:436
  22.1 0.6 collective-permute-start.3
  22.7 1.5 %prepare.1.prop.refs_4_.refs_2_ = f32[2,256,256]{2,1,0:T(8,128)S(1)} custom-call(f32[256,256]{1,0:T(8,128)S(1)} %copy-done.5, bf16[2,256,256]{2,1,0:T(8,128)(2,1)S(1)} %copy-done.4), custom_call_target="tpu_custom_call" | custom-call | tf_op jit(solution)/shard_map/prepare/pallas_call | solution.py:439
  24.1 0.0 collective-permute-done.1.halo
  24.2 2.3 %shard_map.122 = (f32[4,2,256,256]{3,2,1,0:T(8,128)S(1)}, f32[4,2,256,256]{3,2,1,0:T(8,128)S(1)}, f32[2,256,256]{2,1,0:T(8,128)S(1)}) custom-call(s32[3]{0:T(128)S(1)} %pad_add_fusion.place, s32[4]{0:T(128)S(1)} %copy-done.7, s32[4]{0:T(128)S(1)} %copy-done.8, f32[2,256,384]{2,1,0:T(8,128)S(1)} %get-tuple-element.29.own, ...), custom_call_target="tpu_custom_call" | custom-call | tf_op jit(solution)/shard_map/pallas_call | solution.py:469
  26.6 0.0 collective-permute-done.7.refs_3_
  26.6 2.6 %shard_map.123 = (f32[4,2,256,256]{3,2,1,0:T(8,128)S(1)}, f32[4,2,256,256]{3,2,1,0:T(8,128)S(1)}) custom-call(s32[3]{0:T(128)S(1)} %pad_add_fusion.place, f32[2,256,256]{2,1,0:T(8,128)S(1)} %get-tuple-element.30.window.window0, f32[2,128,256]{2,1,0:T(8,128)S(1)} %collective-permute-done.4.refs_0_, ...), custom_call_target="tpu_custom_call", output_to_operand_aliasing={{0}: (10, {}), {1}: (11, {})} | custom-call | tf_op jit(solution)/shard_map/pallas_call | solution.py:476
  29.2 1.9 %shard_map.124 = (f32[4,2,256,256]{3,2,1,0:T(8,128)S(1)}, f32[4,2,256,256]{3,2,1,0:T(8,128)S(1)}) custom-call(s32[3]{0:T(128)S(1)} %pad_add_fusion.place, f32[2,256,256]{2,1,0:T(8,128)S(1)} %get-tuple-element.30.window.window0, f32[2,128,256]{2,1,0:T(8,128)S(1)} %collective-permute-done.2.refs_0_, ...), custom_call_target="tpu_custom_call", output_to_operand_aliasing={{0}: (8, {}), {1}: (9, {})} | custom-call | tf_op jit(solution)/shard_map/pallas_call | solution.py:476
  31.0 0.0 collective-permute-done.halo
  31.1 0.0 copy-start.3
  31.1 4.3 %second.1 = (f32[4,2,256,256]{3,2,1,0:T(8,128)S(1)}, f32[4,2,256,256]{3,2,1,0:T(8,128)S(1)}, f32[256,256]{1,0:T(8,128)S(1)}, f32[2,256,256]{2,1,0:T(8,128)S(1)}) custom-call(s32[3]{0:T(128)S(1)} %pad_add_fusion.place, s32[4]{0:T(128)S(1)} %copy-done.7, s32[4]{0:T(128)S(1)} %copy-done.8, f32[2,256,384]{2,1,0:T(8,128)S(1)} %get-tuple-element.28.own, ...), custom_call_target="tpu_custom_call" | custom-call | tf_op jit(solution)/shard_map/second/pallas_call | solution.py:484
  35.3 4.1 %collective-permute-start.8 = (f32[256,256]{1,0:T(8,128)S(1)}, f32[256,256]{1,0:T(8,128)S(1)}, u32[]{:S(2)}, u32[]{:S(2)}) collective-permute-start(f32[256,256]{1,0:T(8,128)S(1)} %get-tuple-element.41.power), channel_id=1, source_target_pairs={{0,1},{1,0},{2,3},{3,2},{4,5},{5,4},{6,7},{7,6},{8,9},{9,8},{10,11... | collective-permute-start | bytes 786440 | tf_op jit(solution)/shard_map/ppermute | solution.py:494
  39.5 1.2 target.1.measured
  41.3 4.7 %collective-permute-done.8.power_other = f32[256,256]{1,0:T(8,128)S(1)} collective-permute-done((f32[256,256]{1,0:T(8,128)S(1)}, f32[256,256]{1,0:T(8,128)S(1)}, u32[]{:S(2)}, u32[]{:S(2)}) %collective-permute-start.8) | collective-permute-done | bytes 262176 | tf_op jit(solution)/shard_map/ppermute | solution.py:494
  45.9 7.6 %third.1 = (f32[2,2,32,256]{3,2,1,0:T(8,128)S(1)}, f32[2,2,32,256]{3,2,1,0:T(8,128)S(1)}, f32[2,2,32,256]{3,2,1,0:T(8,128)S(1)}, f32[2,2,32,256]{3,2,1,0:T(8,128...) custom-call(s32[3]{0:T(128)S(1)} %pad_add_fusion.place, ...), custom_call_target="tpu_custom_call" | custom-call | tf_op jit(solution)/shard_map/third/pallas_call | solution.py:498
  53.6 0.1 collective-permute-start.24
  53.7 2.6 %collective-permute-done.24 = f32[8,4,2,16,256]{4,3,2,1,0:T(8,128)S(1)} collective-permute-done((f32[8,4,2,16,256]{4,3,2,1,0:T(8,128)S(1)}, f32[8,4,2,16,256]{4,3,2,1,0:T(8,128)S(1)}, u32[]{:S(2)}, u32[]{:S(2)}) %collective-permute-start.24) | collective-permute-done | bytes 1048608 | tf_op jit(solution)/shard_map/ppermute | solution.py:509
  56.3 1.2 add.7
  57.5 8.2 %all-to-all-start = ((f32[32,2,16,256]{3,2,1,0:T(8,128)}), f32[32,2,16,256]{3,2,1,0:T(8,128)S(1)}, u32[]{:S(2)}, u32[]{:S(2)}) async-start(f32[32,2,16,256]{3,2,1,0:T(8,128)} %bitcast.3), calls=%async_computation | async-start | bytes 2097152 | tf_op jit(solution)/shard_map/all_to_all | solution.py:514
  65.8 1.9 %collective-permute-start.10 = (f32[2,2,32,256]{3,2,1,0:T(8,128)S(1)}, f32[2,2,32,256]{3,2,1,0:T(8,128)S(1)}, u32[]{:S(2)}, u32[]{:S(2)}) collective-permute-start(f32[2,2,32,256]{3,2,1,0:T(8,128)S(1)} %get-tuple-element.44), channel_id=1, source_target_pairs={{0,2},{1,3},{2,4},{3,5},{4,6},{5,7},{6,0},{7,1},{8,10},{9,11},{10,... | collective-permute-start | bytes 393224 | tf_op jit(solution)/shard_map/ppermute | solution.py:512
  67.6 4.5 %collective-permute-start.11 = (f32[2,2,32,256]{3,2,1,0:T(8,128)S(1)}, f32[2,2,32,256]{3,2,1,0:T(8,128)S(1)}, u32[]{:S(2)}, u32[]{:S(2)}) collective-permute-start(f32[2,2,32,256]{3,2,1,0:T(8,128)S(1)} %get-tuple-element.45), channel_id=1, source_target_pairs={{0,3},{1,4},{2,5},{3,6},{4,7},{5,0},{6,1},{7,2},{8,11},{9,12},{10,... | collective-permute-start | bytes 393224 | tf_op jit(solution)/shard_map/ppermute | solution.py:512
  72.1 1.4 %collective-permute-start.12 = (f32[2,2,32,256]{3,2,1,0:T(8,128)S(1)}, f32[2,2,32,256]{3,2,1,0:T(8,128)S(1)}, u32[]{:S(2)}, u32[]{:S(2)}) collective-permute-start(f32[2,2,32,256]{3,2,1,0:T(8,128)S(1)} %get-tuple-element.46), channel_id=1, source_target_pairs={{0,4},{1,5},{2,6},{3,7},{4,0},{5,1},{6,2},{7,3},{8,12},{9,13},{10,... | collective-permute-start | bytes 393224 | tf_op jit(solution)/shard_map/ppermute | solution.py:512
  73.5 2.7 %collective-permute-start.13 = (f32[2,2,32,256]{3,2,1,0:T(8,128)S(1)}, f32[2,2,32,256]{3,2,1,0:T(8,128)S(1)}, u32[]{:S(2)}, u32[]{:S(2)}) collective-permute-start(f32[2,2,32,256]{3,2,1,0:T(8,128)S(1)} %get-tuple-element.47), channel_id=1, source_target_pairs={{0,5},{1,6},{2,7},{3,0},{4,1},{5,2},{6,3},{7,4},{8,13},{9,14},{10,... | collective-permute-start | bytes 393224 | tf_op jit(solution)/shard_map/ppermute | solution.py:512
  76.2 1.5 %collective-permute-start.14 = (f32[2,2,32,256]{3,2,1,0:T(8,128)S(1)}, f32[2,2,32,256]{3,2,1,0:T(8,128)S(1)}, u32[]{:S(2)}, u32[]{:S(2)}) collective-permute-start(f32[2,2,32,256]{3,2,1,0:T(8,128)S(1)} %get-tuple-element.48), channel_id=1, source_target_pairs={{0,6},{1,7},{2,0},{3,1},{4,2},{5,3},{6,4},{7,5},{8,14},{9,15},{10,... | collective-permute-start | bytes 393224 | tf_op jit(solution)/shard_map/ppermute | solution.py:512
  77.7 6.4 %collective-permute-done.10.refs_2_ = f32[2,2,32,256]{3,2,1,0:T(8,128)S(1)} collective-permute-done((f32[2,2,32,256]{3,2,1,0:T(8,128)S(1)}, f32[2,2,32,256]{3,2,1,0:T(8,128)S(1)}, u32[]{:S(2)}, u32[]{:S(2)}) %collective-permute-start.10) | collective-permute-done | bytes 131104 | tf_op jit(solution)/shard_map/ppermute | solution.py:512
  84.1 4.1 %collective-permute-start.15 = (f32[2,2,32,256]{3,2,1,0:T(8,128)S(1)}, f32[2,2,32,256]{3,2,1,0:T(8,128)S(1)}, u32[]{:S(2)}, u32[]{:S(2)}) collective-permute-start(f32[2,2,32,256]{3,2,1,0:T(8,128)S(1)} %get-tuple-element.49), channel_id=1, source_target_pairs={{0,7},{1,0},{2,1},{3,2},{4,3},{5,4},{6,5},{7,6},{8,15},{9,8},{10,9... | collective-permute-start | bytes 393224 | tf_op jit(solution)/shard_map/ppermute | solution.py:512
  88.2 3.0 %collective-permute-done.11.refs_3_ = f32[2,2,32,256]{3,2,1,0:T(8,128)S(1)} collective-permute-done((f32[2,2,32,256]{3,2,1,0:T(8,128)S(1)}, f32[2,2,32,256]{3,2,1,0:T(8,128)S(1)}, u32[]{:S(2)}, u32[]{:S(2)}) %collective-permute-start.11) | collective-permute-done | bytes 131104 | tf_op jit(solution)/shard_map/ppermute | solution.py:512
  91.2 1.1 collective-permute-done.13.refs_5_
  92.3 0.0 collective-permute-done.14.refs_6_
  92.3 2.2 %collective-permute-done.15.refs_7_ = f32[2,2,32,256]{3,2,1,0:T(8,128)S(1)} collective-permute-done((f32[2,2,32,256]{3,2,1,0:T(8,128)S(1)}, f32[2,2,32,256]{3,2,1,0:T(8,128)S(1)}, u32[]{:S(2)}, u32[]{:S(2)}) %collective-permute-start.15) | collective-permute-done | bytes 131104 | tf_op jit(solution)/shard_map/ppermute | solution.py:512
  94.5 5.3 %collective-permute-done.9.refs_1_ = f32[2,2,32,256]{3,2,1,0:T(8,128)S(1)} collective-permute-done((f32[2,2,32,256]{3,2,1,0:T(8,128)S(1)}, f32[2,2,32,256]{3,2,1,0:T(8,128)S(1)}, u32[]{:S(2)}, u32[]{:S(2)}) %collective-permute-start.9) | collective-permute-done | bytes 131104 | tf_op jit(solution)/shard_map/ppermute | solution.py:512
  99.8 0.9 gather.1
  100.6 1.3 collective-permute-start.16
  102.0 0.0 all-to-all-done.spread
  102.0 0.9 psum.1
  102.9 6.1 %all-to-all-start.1 = ((f32[16,2,16,256]{3,2,1,0:T(8,128)}), f32[16,2,16,256]{3,2,1,0:T(8,128)S(1)}, u32[]{:S(2)}, u32[]{:S(2)}) async-start(f32[16,2,16,256]{3,2,1,0:T(8,128)} %psum.1), calls=%async_computation.1 | async-start | bytes 1048576 | tf_op jit(solution)/shard_map/all_to_all | solution.py:537
  109.0 0.8 collective-permute-start.17
  109.8 3.8 %collective-permute-start.19 = (f32[2,2,32,384]{3,2,1,0:T(8,128)S(1)}, f32[2,2,32,384]{3,2,1,0:T(8,128)S(1)}, u32[]{:S(2)}, u32[]{:S(2)}) collective-permute-start(f32[2,2,32,384]{3,2,1,0:T(8,128)S(1)} %add.6.refs_0_), channel_id=1, source_target_pairs={{0,3},{1,4},{2,5},{3,6},{4,7},{5,0},{6,1},{7,2},{8,11},{9,12},{10,... | collective-permute-start | bytes 589832 | tf_op jit(solution)/shard_map/ppermute | solution.py:528
  113.6 2.5 %collective-permute-start.20 = (f32[2,2,32,384]{3,2,1,0:T(8,128)S(1)}, f32[2,2,32,384]{3,2,1,0:T(8,128)S(1)}, u32[]{:S(2)}, u32[]{:S(2)}) collective-permute-start(f32[2,2,32,384]{3,2,1,0:T(8,128)S(1)} %add.6.refs_0_), channel_id=1, source_target_pairs={{0,4},{1,5},{2,6},{3,7},{4,0},{5,1},{6,2},{7,3},{8,12},{9,13},{10,... | collective-permute-start | bytes 589832 | tf_op jit(solution)/shard_map/ppermute | solution.py:528
  116.1 1.8 %collective-permute-start.21 = (f32[2,2,32,384]{3,2,1,0:T(8,128)S(1)}, f32[2,2,32,384]{3,2,1,0:T(8,128)S(1)}, u32[]{:S(2)}, u32[]{:S(2)}) collective-permute-start(f32[2,2,32,384]{3,2,1,0:T(8,128)S(1)} %add.6.refs_0_), channel_id=1, source_target_pairs={{0,5},{1,6},{2,7},{3,0},{4,1},{5,2},{6,3},{7,4},{8,13},{9,14},{10,... | collective-permute-start | bytes 589832 | tf_op jit(solution)/shard_map/ppermute | solution.py:528
  117.9 6.0 %collective-permute-done.17.refs_1_ = f32[2,2,32,384]{3,2,1,0:T(8,128)S(1)} collective-permute-done((f32[2,2,32,384]{3,2,1,0:T(8,128)S(1)}, f32[2,2,32,384]{3,2,1,0:T(8,128)S(1)}, u32[]{:S(2)}, u32[]{:S(2)}) %collective-permute-start.17) | collective-permute-done | bytes 196640 | tf_op jit(solution)/shard_map/ppermute | solution.py:528
  124.0 5.0 %collective-permute-start.22 = (f32[2,2,32,384]{3,2,1,0:T(8,128)S(1)}, f32[2,2,32,384]{3,2,1,0:T(8,128)S(1)}, u32[]{:S(2)}, u32[]{:S(2)}) collective-permute-start(f32[2,2,32,384]{3,2,1,0:T(8,128)S(1)} %add.6.refs_0_), channel_id=1, source_target_pairs={{0,6},{1,7},{2,0},{3,1},{4,2},{5,3},{6,4},{7,5},{8,14},{9,15},{10,... | collective-permute-start | bytes 589832 | tf_op jit(solution)/shard_map/ppermute | solution.py:528
  128.9 3.4 %collective-permute-start.23 = (f32[2,2,32,384]{3,2,1,0:T(8,128)S(1)}, f32[2,2,32,384]{3,2,1,0:T(8,128)S(1)}, u32[]{:S(2)}, u32[]{:S(2)}) collective-permute-start(f32[2,2,32,384]{3,2,1,0:T(8,128)S(1)} %add.6.refs_0_), channel_id=1, source_target_pairs={{0,7},{1,0},{2,1},{3,2},{4,3},{5,4},{6,5},{7,6},{8,15},{9,8},{10,9... | collective-permute-start | bytes 589832 | tf_op jit(solution)/shard_map/ppermute | solution.py:528
  132.4 0.9 collective-permute-done.19.refs_3_
  133.3 0.9 collective-permute-done.21.refs_5_
  134.2 4.1 %collective-permute-done.23.refs_7_ = f32[2,2,32,384]{3,2,1,0:T(8,128)S(1)} collective-permute-done((f32[2,2,32,384]{3,2,1,0:T(8,128)S(1)}, f32[2,2,32,384]{3,2,1,0:T(8,128)S(1)}, u32[]{:S(2)}, u32[]{:S(2)}) %collective-permute-start.23) | collective-permute-done | bytes 196640 | tf_op jit(solution)/shard_map/ppermute | solution.py:528
  138.3 1.7 %join.1 = f32[2,2,256,384]{3,2,1,0:T(8,128)} custom-call(s32[3]{0:T(128)S(1)} %pad_add_fusion.place, f32[2,2,32,384]{3,2,1,0:T(8,128)S(1)} %add.6.refs_0_, f32[2,2,32,384]{3,2,1,0:T(8,128)S(1)} %collective-permute-done.17.refs_1_, f32[2,2,32,384]{3,2,1,0:T(8,128)S(1)} %collective-permute-done.18.refs_2_, ...), custom_call_target="tpu_custom_call" | custom-call | tf_op jit(solution)/shard_map/join/pallas_call | solution.py:538
  140.1 0.8 copy.17
  (23 shorter events, 0.1 us)
Async XLA Ops:
  0.6 22.1 %copy-start.4 = (bf16[2,256,256]{2,1,0:T(8,128)(2,1)S(1)}, bf16[2,256,256]{2,1,0:T(8,128)(2,1)}, u32[]{:S(2)}) copy-start(bf16[2,256,256]{2,1,0:T(8,128)(2,1)} %constant.22.clone.picks) | copy-start | bytes 786436
  0.6 23.5 %copy-start = (bf16[4,256,256]{2,1,0:T(8,128)(2,1)S(1)}, bf16[4,256,256]{2,1,0:T(8,128)(2,1)}, u32[]{:S(2)}) copy-start(bf16[4,256,256]{2,1,0:T(8,128)(2,1)} %constant.19.clone.tables.refs_5_.refs_3_) | copy-start | bytes 1572868
  0.7 23.5 %copy-start.6 = (f32[2,8,128]{2,1,0:T(8,128)S(1)}, f32[2,8,128]{2,1,0:T(8,128)}, u32[]{:S(2)}) copy-start(f32[2,8,128]{2,1,0:T(8,128)} %constant.20.clone.lane.refs_6_.refs_4_) | copy-start | bytes 24580
  0.7 23.5 %copy-start.1 = (f32[2,128,128]{2,1,0:T(8,128)S(1)}, f32[2,128,128]{2,1,0:T(8,128)}, u32[]{:S(2)}) copy-start(f32[2,128,128]{2,1,0:T(8,128)} %constant.21.clone.row_table.refs_7_.refs_5_) | copy-start | bytes 393220
  0.7 23.5 %copy-start.2 = (f32[1,2,256,256]{3,2,1,0:T(8,128)S(1)}, f32[1,2,256,256]{3,2,1,0:T(8,128)}, u32[]{:S(2)}) copy-start(f32[1,2,256,256]{3,2,1,0:T(8,128)} %probe.3) | copy-start | bytes 1572868
  0.7 22.0 %copy-start.5 = (f32[256,256]{1,0:T(8,128)S(1)}, f32[256,256]{1,0:T(8,128)}, u32[]{:S(2)}) copy-start(f32[256,256]{1,0:T(8,128)} %phase.1) | copy-start | bytes 786436
  0.7 23.5 %copy-start.7 = (s32[4]{0:T(128)S(1)}, s32[4]{0:T(128)}, u32[]{:S(2)}) copy-start(s32[4]{0:T(128)} %row_off.7) | copy-start | bytes 52
  0.7 23.5 %copy-start.8 = (s32[4]{0:T(128)S(1)}, s32[4]{0:T(128)}, u32[]{:S(2)}) copy-start(s32[4]{0:T(128)} %col_off.7) | copy-start | bytes 52
  2.8 21.3 %collective-permute-start.1 = (f32[2,256,384]{2,1,0:T(8,128)S(1)}, f32[2,256,384]{2,1,0:T(8,128)S(1)}, u32[]{:S(2)}, u32[]{:S(2)}) collective-permute-start(f32[2,256,384]{2,1,0:T(8,128)S(1)} %get-tuple-element.29.own), channel_id=1, source_target_pairs={{8,0},{16,8},{24,16},{32,24},{40,32},{48,40},{56,48},{64,56},{72,6... | collective-permute-start | bytes 2359304 | tf_op jit(solution)/shard_map/ppermute | solution.py:431
  4.1 26.9 %collective-permute-start = (f32[2,256,384]{2,1,0:T(8,128)S(1)}, f32[2,256,384]{2,1,0:T(8,128)S(1)}, u32[]{:S(2)}, u32[]{:S(2)}) collective-permute-start(f32[2,256,384]{2,1,0:T(8,128)S(1)} %get-tuple-element.28.own), channel_id=1, source_target_pairs={{8,0},{16,8},{24,16},{32,24},{40,32},{48,40},{56,48},{64,56},{72,6... | collective-permute-start | bytes 2359304 | tf_op jit(solution)/shard_map/ppermute | solution.py:432
  5.4 9.5 %collective-permute-start.4 = (f32[2,128,256]{2,1,0:T(8,128)S(1)}, f32[2,128,256]{2,1,0:T(8,128)S(1)}, u32[]{:S(2)}, u32[]{:S(2)}) collective-permute-start(f32[2,128,256]{2,1,0:T(8,128)S(1)} %get-tuple-element.31), channel_id=1, source_target_pairs={{0,2},{2,4},{4,6},{6,0},{1,3},{3,5},{5,7},{7,1},{8,10},{10,12},{12... | collective-permute-start | bytes 786440 | tf_op jit(solution)/shard_map/ppermute | solution.py:436
  7.2 8.7 %collective-permute-start.5 = (f32[2,128,256]{2,1,0:T(8,128)S(1)}, f32[2,128,256]{2,1,0:T(8,128)S(1)}, u32[]{:S(2)}, u32[]{:S(2)}) collective-permute-start(f32[2,128,256]{2,1,0:T(8,128)S(1)} %get-tuple-element.31), channel_id=1, source_target_pairs={{0,6},{2,0},{4,2},{6,4},{1,7},{3,1},{5,3},{7,5},{8,14},{10,8},{12,... | collective-permute-start | bytes 786440 | tf_op jit(solution)/shard_map/ppermute | solution.py:436
  8.7 13.3 %collective-permute-start.2 = (f32[2,128,256]{2,1,0:T(8,128)S(1)}, f32[2,128,256]{2,1,0:T(8,128)S(1)}, u32[]{:S(2)}, u32[]{:S(2)}) collective-permute-start(f32[2,128,256]{2,1,0:T(8,128)S(1)} %get-tuple-element.31), channel_id=1, source_target_pairs={{0,4},{2,6},{4,0},{6,2},{1,5},{3,7},{5,1},{7,3},{8,12},{10,14},{12... | collective-permute-start | bytes 786440 | tf_op jit(solution)/shard_map/ppermute | solution.py:436
  14.9 11.6 %collective-permute-start.6 = (f32[2,128,256]{2,1,0:T(8,128)S(1)}, f32[2,128,256]{2,1,0:T(8,128)S(1)}, u32[]{:S(2)}, u32[]{:S(2)}) collective-permute-start(f32[2,128,256]{2,1,0:T(8,128)S(1)} %collective-permute-done.4.refs_0_), channel_id=1, source_target_pairs={{0,8},{8,0},{1,9},{9,1},{2,10},{10,2},{3,11},{11,3},{4,12},{12,4},... | collective-permute-start | bytes 786440 | tf_op jit(solution)/shard_map/ppermute | solution.py:437
  15.9 10.7 %collective-permute-start.7 = (f32[2,128,256]{2,1,0:T(8,128)S(1)}, f32[2,128,256]{2,1,0:T(8,128)S(1)}, u32[]{:S(2)}, u32[]{:S(2)}) collective-permute-start(f32[2,128,256]{2,1,0:T(8,128)S(1)} %collective-permute-done.5.refs_1_), channel_id=1, source_target_pairs={{0,8},{8,0},{1,9},{9,1},{2,10},{10,2},{3,11},{11,3},{4,12},{12,4},... | collective-permute-start | bytes 786440 | tf_op jit(solution)/shard_map/ppermute | solution.py:437
  22.1 7.1 %collective-permute-start.3 = (f32[2,128,256]{2,1,0:T(8,128)S(1)}, f32[2,128,256]{2,1,0:T(8,128)S(1)}, u32[]{:S(2)}, u32[]{:S(2)}) collective-permute-start(f32[2,128,256]{2,1,0:T(8,128)S(1)} %collective-permute-done.2.refs_0_), channel_id=1, source_target_pairs={{0,8},{8,0},{1,9},{9,1},{2,10},{10,2},{3,11},{11,3},{4,12},{12,4},... | collective-permute-start | bytes 786440 | tf_op jit(solution)/shard_map/ppermute | solution.py:437
  31.1 8.4 %copy-start.3 = (f32[4,256,256]{2,1,0:T(8,128)S(1)}, f32[4,256,256]{2,1,0:T(8,128)}, u32[]{:S(2)}) copy-start(f32[4,256,256]{2,1,0:T(8,128)} %measured.1) | copy-start | bytes 3145732
  35.3 10.6 %collective-permute-start.8 = (f32[256,256]{1,0:T(8,128)S(1)}, f32[256,256]{1,0:T(8,128)S(1)}, u32[]{:S(2)}, u32[]{:S(2)}) collective-permute-start(f32[256,256]{1,0:T(8,128)S(1)} %get-tuple-element.41.power), channel_id=1, source_target_pairs={{0,1},{1,0},{2,3},{3,2},{4,5},{5,4},{6,7},{7,6},{8,9},{9,8},{10,11... | collective-permute-start | bytes 786440 | tf_op jit(solution)/shard_map/ppermute | solution.py:494
  53.6 2.7 %collective-permute-start.24 = (f32[8,4,2,16,256]{4,3,2,1,0:T(8,128)S(1)}, f32[8,4,2,16,256]{4,3,2,1,0:T(8,128)S(1)}, u32[]{:S(2)}, u32[]{:S(2)}) collective-permute-start(f32[8,4,2,16,256]{4,3,2,1,0:T(8,128)S(1)} %get-tuple-element.53), channel_id=1, source_target_pairs={{0,8},{8,0},{1,9},{9,1},{2,10},{10,2},{3,11},{11,3},{4,12},{12,4},... | collective-permute-start | bytes 3145736 | tf_op jit(solution)/shard_map/ppermute | solution.py:509
  57.5 44.4 %all-to-all-start = ((f32[32,2,16,256]{3,2,1,0:T(8,128)}), f32[32,2,16,256]{3,2,1,0:T(8,128)S(1)}, u32[]{:S(2)}, u32[]{:S(2)}) async-start(f32[32,2,16,256]{3,2,1,0:T(8,128)} %bitcast.3), calls=%async_computation | async-start | bytes 2097152 | tf_op jit(solution)/shard_map/all_to_all | solution.py:514
  65.8 18.3 %collective-permute-start.10 = (f32[2,2,32,256]{3,2,1,0:T(8,128)S(1)}, f32[2,2,32,256]{3,2,1,0:T(8,128)S(1)}, u32[]{:S(2)}, u32[]{:S(2)}) collective-permute-start(f32[2,2,32,256]{3,2,1,0:T(8,128)S(1)} %get-tuple-element.44), channel_id=1, source_target_pairs={{0,2},{1,3},{2,4},{3,5},{4,6},{5,7},{6,0},{7,1},{8,10},{9,11},{10,... | collective-permute-start | bytes 393224 | tf_op jit(solution)/shard_map/ppermute | solution.py:512
  67.6 23.6 %collective-permute-start.11 = (f32[2,2,32,256]{3,2,1,0:T(8,128)S(1)}, f32[2,2,32,256]{3,2,1,0:T(8,128)S(1)}, u32[]{:S(2)}, u32[]{:S(2)}) collective-permute-start(f32[2,2,32,256]{3,2,1,0:T(8,128)S(1)} %get-tuple-element.45), channel_id=1, source_target_pairs={{0,3},{1,4},{2,5},{3,6},{4,7},{5,0},{6,1},{7,2},{8,11},{9,12},{10,... | collective-permute-start | bytes 393224 | tf_op jit(solution)/shard_map/ppermute | solution.py:512
  72.1 19.1 %collective-permute-start.12 = (f32[2,2,32,256]{3,2,1,0:T(8,128)S(1)}, f32[2,2,32,256]{3,2,1,0:T(8,128)S(1)}, u32[]{:S(2)}, u32[]{:S(2)}) collective-permute-start(f32[2,2,32,256]{3,2,1,0:T(8,128)S(1)} %get-tuple-element.46), channel_id=1, source_target_pairs={{0,4},{1,5},{2,6},{3,7},{4,0},{5,1},{6,2},{7,3},{8,12},{9,13},{10,... | collective-permute-start | bytes 393224 | tf_op jit(solution)/shard_map/ppermute | solution.py:512
  73.5 18.7 %collective-permute-start.13 = (f32[2,2,32,256]{3,2,1,0:T(8,128)S(1)}, f32[2,2,32,256]{3,2,1,0:T(8,128)S(1)}, u32[]{:S(2)}, u32[]{:S(2)}) collective-permute-start(f32[2,2,32,256]{3,2,1,0:T(8,128)S(1)} %get-tuple-element.47), channel_id=1, source_target_pairs={{0,5},{1,6},{2,7},{3,0},{4,1},{5,2},{6,3},{7,4},{8,13},{9,14},{10,... | collective-permute-start | bytes 393224 | tf_op jit(solution)/shard_map/ppermute | solution.py:512
  76.2 16.1 %collective-permute-start.14 = (f32[2,2,32,256]{3,2,1,0:T(8,128)S(1)}, f32[2,2,32,256]{3,2,1,0:T(8,128)S(1)}, u32[]{:S(2)}, u32[]{:S(2)}) collective-permute-start(f32[2,2,32,256]{3,2,1,0:T(8,128)S(1)} %get-tuple-element.48), channel_id=1, source_target_pairs={{0,6},{1,7},{2,0},{3,1},{4,2},{5,3},{6,4},{7,5},{8,14},{9,15},{10,... | collective-permute-start | bytes 393224 | tf_op jit(solution)/shard_map/ppermute | solution.py:512
  84.1 10.4 %collective-permute-start.15 = (f32[2,2,32,256]{3,2,1,0:T(8,128)S(1)}, f32[2,2,32,256]{3,2,1,0:T(8,128)S(1)}, u32[]{:S(2)}, u32[]{:S(2)}) collective-permute-start(f32[2,2,32,256]{3,2,1,0:T(8,128)S(1)} %get-tuple-element.49), channel_id=1, source_target_pairs={{0,7},{1,0},{2,1},{3,2},{4,3},{5,4},{6,5},{7,6},{8,15},{9,8},{10,9... | collective-permute-start | bytes 393224 | tf_op jit(solution)/shard_map/ppermute | solution.py:512
  91.2 8.6 %collective-permute-start.9 = (f32[2,2,32,256]{3,2,1,0:T(8,128)S(1)}, f32[2,2,32,256]{3,2,1,0:T(8,128)S(1)}, u32[]{:S(2)}, u32[]{:S(2)}) collective-permute-start(f32[2,2,32,256]{3,2,1,0:T(8,128)S(1)} %get-tuple-element.43), channel_id=1, source_target_pairs={{0,1},{1,2},{2,3},{3,4},{4,5},{5,6},{6,7},{7,0},{8,9},{9,10},{10,1... | collective-permute-start | bytes 393224 | tf_op jit(solution)/shard_map/ppermute | solution.py:512
  100.6 8.3 %collective-permute-start.16 = (f32[2,2,32,384]{3,2,1,0:T(8,128)S(1)}, f32[2,2,32,384]{3,2,1,0:T(8,128)S(1)}, u32[]{:S(2)}, u32[]{:S(2)}) collective-permute-start(f32[2,2,32,384]{3,2,1,0:T(8,128)S(1)} %get-tuple-element.51), channel_id=1, source_target_pairs={{0,8},{8,16},{16,24},{24,32},{32,40},{40,48},{48,56},{56,64},{64,7... | collective-permute-start | bytes 589832 | tf_op jit(solution)/shard_map/ppermute | solution.py:523
  102.9 37.2 %all-to-all-start.1 = ((f32[16,2,16,256]{3,2,1,0:T(8,128)}), f32[16,2,16,256]{3,2,1,0:T(8,128)S(1)}, u32[]{:S(2)}, u32[]{:S(2)}) async-start(f32[16,2,16,256]{3,2,1,0:T(8,128)} %psum.1), calls=%async_computation.1 | async-start | bytes 1048576 | tf_op jit(solution)/shard_map/all_to_all | solution.py:537
  109.0 15.0 %collective-permute-start.17 = (f32[2,2,32,384]{3,2,1,0:T(8,128)S(1)}, f32[2,2,32,384]{3,2,1,0:T(8,128)S(1)}, u32[]{:S(2)}, u32[]{:S(2)}) collective-permute-start(f32[2,2,32,384]{3,2,1,0:T(8,128)S(1)} %add.6.refs_0_), channel_id=1, source_target_pairs={{0,1},{1,2},{2,3},{3,4},{4,5},{5,6},{6,7},{7,0},{8,9},{9,10},{10,1... | collective-permute-start | bytes 589832 | tf_op jit(solution)/shard_map/ppermute | solution.py:528
  109.8 19.2 %collective-permute-start.18 = (f32[2,2,32,384]{3,2,1,0:T(8,128)S(1)}, f32[2,2,32,384]{3,2,1,0:T(8,128)S(1)}, u32[]{:S(2)}, u32[]{:S(2)}) collective-permute-start(f32[2,2,32,384]{3,2,1,0:T(8,128)S(1)} %add.6.refs_0_), channel_id=1, source_target_pairs={{0,2},{1,3},{2,4},{3,5},{4,6},{5,7},{6,0},{7,1},{8,10},{9,11},{10,... | collective-permute-start | bytes 589832 | tf_op jit(solution)/shard_map/ppermute | solution.py:528
  109.8 23.5 %collective-permute-start.19 = (f32[2,2,32,384]{3,2,1,0:T(8,128)S(1)}, f32[2,2,32,384]{3,2,1,0:T(8,128)S(1)}, u32[]{:S(2)}, u32[]{:S(2)}) collective-permute-start(f32[2,2,32,384]{3,2,1,0:T(8,128)S(1)} %add.6.refs_0_), channel_id=1, source_target_pairs={{0,3},{1,4},{2,5},{3,6},{4,7},{5,0},{6,1},{7,2},{8,11},{9,12},{10,... | collective-permute-start | bytes 589832 | tf_op jit(solution)/shard_map/ppermute | solution.py:528
  113.6 19.6 %collective-permute-start.20 = (f32[2,2,32,384]{3,2,1,0:T(8,128)S(1)}, f32[2,2,32,384]{3,2,1,0:T(8,128)S(1)}, u32[]{:S(2)}, u32[]{:S(2)}) collective-permute-start(f32[2,2,32,384]{3,2,1,0:T(8,128)S(1)} %add.6.refs_0_), channel_id=1, source_target_pairs={{0,4},{1,5},{2,6},{3,7},{4,0},{5,1},{6,2},{7,3},{8,12},{9,13},{10,... | collective-permute-start | bytes 589832 | tf_op jit(solution)/shard_map/ppermute | solution.py:528
  116.1 18.0 %collective-permute-start.21 = (f32[2,2,32,384]{3,2,1,0:T(8,128)S(1)}, f32[2,2,32,384]{3,2,1,0:T(8,128)S(1)}, u32[]{:S(2)}, u32[]{:S(2)}) collective-permute-start(f32[2,2,32,384]{3,2,1,0:T(8,128)S(1)} %add.6.refs_0_), channel_id=1, source_target_pairs={{0,5},{1,6},{2,7},{3,0},{4,1},{5,2},{6,3},{7,4},{8,13},{9,14},{10,... | collective-permute-start | bytes 589832 | tf_op jit(solution)/shard_map/ppermute | solution.py:528
  124.0 10.2 %collective-permute-start.22 = (f32[2,2,32,384]{3,2,1,0:T(8,128)S(1)}, f32[2,2,32,384]{3,2,1,0:T(8,128)S(1)}, u32[]{:S(2)}, u32[]{:S(2)}) collective-permute-start(f32[2,2,32,384]{3,2,1,0:T(8,128)S(1)} %add.6.refs_0_), channel_id=1, source_target_pairs={{0,6},{1,7},{2,0},{3,1},{4,2},{5,3},{6,4},{7,5},{8,14},{9,15},{10,... | collective-permute-start | bytes 589832 | tf_op jit(solution)/shard_map/ppermute | solution.py:528
  128.9 9.4 %collective-permute-start.23 = (f32[2,2,32,384]{3,2,1,0:T(8,128)S(1)}, f32[2,2,32,384]{3,2,1,0:T(8,128)S(1)}, u32[]{:S(2)}, u32[]{:S(2)}) collective-permute-start(f32[2,2,32,384]{3,2,1,0:T(8,128)S(1)} %add.6.refs_0_), channel_id=1, source_target_pairs={{0,7},{1,0},{2,1},{3,2},{4,3},{5,4},{6,5},{7,6},{8,15},{9,8},{10,9... | collective-permute-start | bytes 589832 | tf_op jit(solution)/shard_map/ppermute | solution.py:528
